TPU v7x, 256 devices: a whole 4x4x8 slice. The times are simulated.
256 devices in a mesh: node: 32 (over x_hi, z, core), feat: 8 (over x_lo, y).
Axes of the slice: x: 4 (x_hi: 2, x_lo: 2; x = x_hi * 2 + x_lo), y: 4, z: 8, core: 2. Of those that a mesh axis runs over, the one named last changes fastest.
Arguments:
- features: bfloat16 [512, 131072], P('feat', 'node'), may hold values from -6 to 6
- tiles: bfloat16 [7680, 128, 128], P('node')
- tile_rows: int32 [7680], P('node'), may hold values from 0 to 31
- tile_cols: int32 [7680], P('node'), may hold values from 0 to 31
- counts: int32 [160], P('node'), may hold values from 12 to 48, as said below
- weight_one: bfloat16 [512, 512], replicated, may hold values from -0.25 to 0.25
- weight_two: bfloat16 [512, 512], replicated, may hold values from -0.25 to 0.25
- cotangent: bfloat16 [512, 131072], P('feat', 'node'), may hold values from -6 to 6
Outputs:
- layer_out: bfloat16 [512, 131072], P('feat', 'node')
- feature_grad: bfloat16 [512, 131072], P('feat', 'node')
- weight_one_grad: float32 [512, 512], P('feat')
- weight_two_grad: float32 [512, 512], P('feat')
Inputs may be any that keep to these rules, and one draw needn't show every extreme that they name: Slots at or beyond counts[p * 5 + o] are not part of A. Some entry equals 48 in every draw.
All inputs are finite; a program needn't handle non-finite values.
Results may differ from a plain program's by a relative error of at most 0.0051.
Values may be sent and summed in bfloat16 or wider, within the bound.
A program may use at most 128 MiB of HBM per device.

v0:
```python
import jax
import jax.numpy as jnp
from jax import lax
from jax.sharding import PartitionSpec as P


def passed_along(value, axis, steps):
    count = lax.axis_size(axis)
    pairs = [(source, (source + steps) % count) for source in range(count)]
    return lax.ppermute(value, axis, pairs)


def forward_term(panel, tile_set, slot_rows, slot_cols, live):
    width, length = panel.shape
    block = tile_set.shape[-1]
    blocks_count = length // block
    pieces = jnp.take(panel.reshape(width, blocks_count, block), slot_cols, axis=1)
    partial_out = jnp.einsum("hsk,srk->hsr", pieces, tile_set, preferred_element_type=jnp.float32)
    selector = (
        (slot_rows[None, :] == jnp.arange(blocks_count, dtype=jnp.int32)[:, None]) & live[None, :]
    ).astype(jnp.float32)
    return jnp.einsum(
        "hsr,bs->hbr", partial_out, selector, precision=lax.Precision.HIGHEST
    ).reshape(width, length)


def backward_term(panel, tile_set, slot_rows, slot_cols, live):
    width, length = panel.shape
    block = tile_set.shape[-1]
    blocks_count = length // block
    pieces = jnp.take(panel.reshape(width, blocks_count, block), slot_rows, axis=1)
    partial_out = jnp.einsum("hsr,srk->hsk", pieces, tile_set, preferred_element_type=jnp.float32)
    selector = (
        (slot_cols[None, :] == jnp.arange(blocks_count, dtype=jnp.int32)[:, None]) & live[None, :]
    ).astype(jnp.float32)
    return jnp.einsum(
        "hsk,bs->hbk", partial_out, selector, precision=lax.Precision.HIGHEST
    ).reshape(width, length)


def slope(back, pre_value):
    sigma = jax.nn.sigmoid(pre_value)
    return (back.astype(jnp.float32) * sigma * (1.0 + pre_value * (1.0 - sigma))).astype(
        jnp.bfloat16
    )


def on_device(features, tiles, tile_rows, tile_cols, counts, weight_one, weight_two, cotangent):
    offsets = counts.shape[0]
    reach = (offsets - 1) // 2
    slots = tile_rows.shape[0] // offsets
    block = tiles.shape[-1]
    tile_set = tiles.reshape(offsets, slots, block, block)
    slot_rows = tile_rows.reshape(offsets, slots)
    slot_cols = tile_cols.reshape(offsets, slots)
    live = jnp.arange(slots, dtype=jnp.int32)[None, :] < counts[:, None]

    def forward_at(panel, offset):
        return forward_term(
            panel, tile_set[offset], slot_rows[offset], slot_cols[offset], live[offset]
        )

    def backward_at(panel, offset):
        return backward_term(
            panel, tile_set[offset], slot_rows[offset], slot_cols[offset], live[offset]
        )

    def aggregate(panel):
        total = forward_at(panel, reach)
        for offset in range(offsets):
            if offset != reach:
                source = passed_along(panel, "node", reach - offset)
                total = total + forward_at(source, offset)
        return total

    def spread(panel):
        total = backward_at(panel, reach)
        for offset in range(offsets):
            if offset != reach:
                total = total + passed_along(backward_at(panel, offset), "node", offset - reach)
        return total

    contract_lead = (((0,), (0,)), ((), ()))
    contract_tail = (((1,), (1,)), ((), ()))

    def to_rows(field):
        return lax.all_to_all(field, "feat", split_axis=1, concat_axis=0, tiled=True)

    def to_features(field):
        return lax.all_to_all(field, "feat", split_axis=0, concat_axis=1, tiled=True)

    agg_rows = to_rows(aggregate(features).astype(jnp.bfloat16))
    pre_rows = lax.dot_general(
        weight_one, agg_rows, contract_lead, preferred_element_type=jnp.float32
    )
    first_act = to_features(jax.nn.silu(pre_rows).astype(jnp.bfloat16))
    second_rows = to_rows(aggregate(first_act).astype(jnp.bfloat16))
    layer_out = to_features(
        lax.dot_general(
            weight_two, second_rows, contract_lead, preferred_element_type=jnp.float32
        ).astype(jnp.bfloat16)
    )
    cot_rows = to_rows(cotangent)
    two_part = lax.dot_general(
        second_rows, cot_rows, contract_tail, preferred_element_type=jnp.float32
    )
    second_back = to_features(
        jnp.dot(weight_two, cot_rows, preferred_element_type=jnp.float32).astype(jnp.bfloat16)
    )
    act_back = to_rows(spread(second_back).astype(jnp.bfloat16))
    pre_back = slope(act_back, pre_rows)
    one_part = lax.dot_general(
        agg_rows, pre_back, contract_tail, preferred_element_type=jnp.float32
    )
    first_back = to_features(
        jnp.dot(weight_one, pre_back, preferred_element_type=jnp.float32).astype(jnp.bfloat16)
    )
    one_rows, two_rows = (
        lax.psum_scatter(one_part, "feat", scatter_dimension=0, tiled=True),
        lax.psum_scatter(two_part, "feat", scatter_dimension=0, tiled=True),
    )
    one_grad, two_grad = lax.psum((one_rows, two_rows), "node")
    feature_grad = spread(first_back).astype(jnp.bfloat16)
    return (layer_out, feature_grad, one_grad, two_grad)


def solution(mesh):
    in_specs = (
        P("feat", "node"),
        P("node", None, None),
        P("node"),
        P("node"),
        P("node"),
        P(),
        P(),
        P("feat", "node"),
    )
    out_specs = (P("feat", "node"), P("feat", "node"), P("feat", None), P("feat", None))
    return jax.shard_map(
        on_device, mesh=mesh, in_specs=in_specs, out_specs=out_specs, check_vma=False
    )
```

profile of v0, /device:TPU:25, one launch (start us, length us, event | category | flops | bytes accessed | tf_op | source)
XLA Modules:
  0.0 608.5 jit_solution(16318424099240862246)
XLA Ops:
  11.4 4.8 collective-permute-start.3
  18.1 4.2 all-to-all-start.4
  26.2 11.5 %all-to-all-done.4 = bf16[64,8,512]{2,0,1:T(8,128)(2,1)S(1)} async-done(((bf16[64,8,512]{2,0,1:T(8,128)(2,1)}), bf16[64,8,512]{2,0,1:T(8,128)(2,1)S(1)}, u32[]{:S(2)}, u32[]{:S(2)}) %all-to-all-start.4) | async-done | bytes 524320 | tf_op jit(solution)/shard_map/all_to_all | solution.py:87
  40.0 5.2 all-to-all-start.5
  50.7 4.1 convolution_bitcast_fusion.18
  54.8 3.7 convolution_bitcast_fusion.17
  61.3 3.0 fusion.36
  66.0 2.6 fusion.43
  74.0 4.0 convolution_bitcast_fusion.15
  103.4 6.9 %collective-permute-start.8 = (f32[64,4096]{1,0:T(8,128)}, f32[64,4096]{1,0:T(8,128)}, u32[]{:S(2)}, u32[]{:S(2)}) collective-permute-start(f32[64,4096]{1,0:T(8,128)} %bitcast.315), channel_id=1, source_target_pairs={{0,240},{8,248},{16,0},{24,8},{32,16},{40,24},{48,32},{56,40},{64,... | collective-permute-start | bytes 3145736 | tf_op jit(solution)/shard_map/ppermute | solution.py:10
  123.3 4.6 all-to-all-start
  133.5 6.3 %collective-permute-done.9 = f32[64,4096]{1,0:T(8,128)} collective-permute-done((f32[64,4096]{1,0:T(8,128)}, f32[64,4096]{1,0:T(8,128)}, u32[]{:S(2)}, u32[]{:S(2)}) %collective-permute-start.9) | collective-permute-done | bytes 1048608 | tf_op jit(solution)/shard_map/ppermute | solution.py:10
  139.8 3.1 fusion.83
  143.8 5.2 all-to-all-start.6
  150.5 3.7 all-to-all-done.6
  156.6 5.3 all-to-all-start.1
  163.2 4.0 all-to-all-done.1
  167.2 5.3 all-to-all-start.7
  174.9 2.7 collective-permute-start.5
  177.6 4.9 collective-permute-start.6
  182.5 9.8 %collective-permute-start.7 = (bf16[64,4096]{1,0:T(8,128)(2,1)}, bf16[64,4096]{1,0:T(8,128)(2,1)}, u32[]{:S(2)}, u32[]{:S(2)}) collective-permute-start(bf16[64,4096]{1,0:T(8,128)(2,1)} %bitcast.115), channel_id=1, source_target_pairs={{0,240},{8,248},{16,0},{24,8},{32,16},{40,24},{48,32},{56,40},{64,... | collective-permute-start | bytes 1572872 | tf_op jit(solution)/shard_map/ppermute | solution.py:10
  205.4 4.0 collective-permute-start.12
  217.5 4.0 convolution_bitcast_fusion.13
  221.6 3.8 convolution_bitcast_fusion.12
  228.1 4.0 fusion.26
  232.2 3.7 convolution_bitcast_fusion.11
  238.7 3.0 fusion.52
  250.9 5.3 all-to-all-start.2
  281.6 5.2 all-to-all-start.3
  286.8 44.9 %reduce-scatter.5.cloned.1.call-done = f32[64,512]{1,0:T(8,128)} async-done(((f32[512,512]{1,0:T(8,128)}), f32[64,512]{1,0:T(8,128)}) %reduce-scatter.5.cloned.1.call-update) | async-done | bytes 131088 | tf_op jit(solution)/shard_map/reduce_scatter | solution.py:120
  331.7 3.8 fusion.79
  336.4 262.2 %all-reduce.3.cloned.1.call-done = (f32[64,512]{1,0:T(8,128)}, f32[64,512]{1,0:T(8,128)}) async-done(((f32[64,512]{1,0:T(8,128)}, f32[64,512]{1,0:T(8,128)}), (f32[64,512]{1,0:T(8,128)}, f32[64,512]{1,0:T(8,128)})) %all-reduce.3.cloned.1.call-update) | async-done | bytes 262160 | tf_op jit(solution)/shard_map/psum | solution.py:122
  (184 shorter events, 144.9 us)
Async XLA Ops:
  7.2 141.8 %copy-start = (bf16[512,512]{1,0:T(8,128)(2,1)S(1)}, bf16[512,512]{1,0:T(8,128)(2,1)}, u32[]{:S(2)}) copy-start(bf16[512,512]{1,0:T(8,128)(2,1)} %param.15) | copy-start | bytes 1572868
  7.2 15.4 %copy-start.16 = (bf16[64,4096]{1,0:T(8,128)(2,1)S(1)}, bf16[64,4096]{1,0:T(8,128)(2,1)}, u32[]{:S(2)}) copy-start(bf16[64,4096]{1,0:T(8,128)(2,1)} %param.10) | copy-start | bytes 1572868
  7.2 15.0 %copy-start.17 = (s32[240]{0:T(256)S(1)}, s32[240]{0:T(256)}, u32[]{:S(2)}) copy-start(s32[240]{0:T(256)} %param.13) | copy-start | bytes 2884
  7.2 15.2 %copy-start.18 = (s32[240]{0:T(256)S(1)}, s32[240]{0:T(256)}, u32[]{:S(2)}) copy-start(s32[240]{0:T(256)} %param.12) | copy-start | bytes 2884
  7.2 38.0 %collective-permute-start = (bf16[64,4096]{1,0:T(8,128)(2,1)}, bf16[64,4096]{1,0:T(8,128)(2,1)}, u32[]{:S(2)}, u32[]{:S(2)}) collective-permute-start(bf16[64,4096]{1,0:T(8,128)(2,1)} %param.10), channel_id=1, source_target_pairs={{0,16},{8,24},{16,32},{24,40},{32,48},{40,56},{48,64},{56,72},{64,... | collective-permute-start | bytes 1572872 | tf_op jit(solution)/shard_map/ppermute | solution.py:10
  8.9 39.0 %collective-permute-start.1 = (bf16[64,4096]{1,0:T(8,128)(2,1)}, bf16[64,4096]{1,0:T(8,128)(2,1)}, u32[]{:S(2)}, u32[]{:S(2)}) collective-permute-start(bf16[64,4096]{1,0:T(8,128)(2,1)} %param.10), channel_id=1, source_target_pairs={{0,8},{8,16},{16,24},{24,32},{32,40},{40,48},{48,56},{56,64},{64,7... | collective-permute-start | bytes 1572872 | tf_op jit(solution)/shard_map/ppermute | solution.py:10
  11.4 47.2 %collective-permute-start.2 = (bf16[64,4096]{1,0:T(8,128)(2,1)}, bf16[64,4096]{1,0:T(8,128)(2,1)}, u32[]{:S(2)}, u32[]{:S(2)}) collective-permute-start(bf16[64,4096]{1,0:T(8,128)(2,1)} %param.10), channel_id=1, source_target_pairs={{0,248},{8,0},{16,8},{24,16},{32,24},{40,32},{48,40},{56,48},{64,5... | collective-permute-start | bytes 1572872 | tf_op jit(solution)/shard_map/ppermute | solution.py:10
  11.4 59.8 %collective-permute-start.3 = (bf16[64,4096]{1,0:T(8,128)(2,1)}, bf16[64,4096]{1,0:T(8,128)(2,1)}, u32[]{:S(2)}, u32[]{:S(2)}) collective-permute-start(bf16[64,4096]{1,0:T(8,128)(2,1)} %param.10), channel_id=1, source_target_pairs={{0,240},{8,248},{16,0},{24,8},{32,16},{40,24},{48,32},{56,40},{64,... | collective-permute-start | bytes 1572872 | tf_op jit(solution)/shard_map/ppermute | solution.py:10
  18.1 19.7 %all-to-all-start.4 = ((bf16[64,8,512]{2,0,1:T(8,128)(2,1)}), bf16[64,8,512]{2,0,1:T(8,128)(2,1)S(1)}, u32[]{:S(2)}, u32[]{:S(2)}) async-start(bf16[64,8,512]{2,0,1:T(8,128)(2,1)} %bitcast.317), calls=%async_computation.4 | async-start | bytes 1048576 | tf_op jit(solution)/shard_map/all_to_all | solution.py:87
  40.0 38.0 %all-to-all-start.5 = ((bf16[8,64,512]{2,1,0:T(8,128)(2,1)}), bf16[8,64,512]{2,1,0:T(8,128)(2,1)}, u32[]{:S(2)}, u32[]{:S(2)}) async-start(bf16[8,64,512]{2,1,0:T(8,128)(2,1)} %bitcast.45), calls=%async_computation.5 | async-start | bytes 1048576 | tf_op jit(solution)/shard_map/all_to_all | solution.py:90
  89.2 44.3 %collective-permute-start.10 = (f32[64,4096]{1,0:T(8,128)}, f32[64,4096]{1,0:T(8,128)}, u32[]{:S(2)}, u32[]{:S(2)}) collective-permute-start(f32[64,4096]{1,0:T(8,128)} %bitcast.313), channel_id=1, source_target_pairs={{0,8},{8,16},{16,24},{24,32},{32,40},{40,48},{48,56},{56,64},{64,7... | collective-permute-start | bytes 3145736 | tf_op jit(solution)/shard_map/ppermute | solution.py:10
  96.2 37.2 %collective-permute-start.11 = (f32[64,4096]{1,0:T(8,128)}, f32[64,4096]{1,0:T(8,128)}, u32[]{:S(2)}, u32[]{:S(2)}) collective-permute-start(f32[64,4096]{1,0:T(8,128)} %bitcast.312), channel_id=1, source_target_pairs={{0,16},{8,24},{16,32},{24,40},{32,48},{40,56},{48,64},{56,72},{64,... | collective-permute-start | bytes 3145736 | tf_op jit(solution)/shard_map/ppermute | solution.py:10
  103.4 30.1 %collective-permute-start.8 = (f32[64,4096]{1,0:T(8,128)}, f32[64,4096]{1,0:T(8,128)}, u32[]{:S(2)}, u32[]{:S(2)}) collective-permute-start(f32[64,4096]{1,0:T(8,128)} %bitcast.315), channel_id=1, source_target_pairs={{0,240},{8,248},{16,0},{24,8},{32,16},{40,24},{48,32},{56,40},{64,... | collective-permute-start | bytes 3145736 | tf_op jit(solution)/shard_map/ppermute | solution.py:10
  117.4 22.4 %collective-permute-start.9 = (f32[64,4096]{1,0:T(8,128)}, f32[64,4096]{1,0:T(8,128)}, u32[]{:S(2)}, u32[]{:S(2)}) collective-permute-start(f32[64,4096]{1,0:T(8,128)} %bitcast.314), channel_id=1, source_target_pairs={{0,248},{8,0},{16,8},{24,16},{32,24},{40,32},{48,40},{56,48},{64,5... | collective-permute-start | bytes 3145736 | tf_op jit(solution)/shard_map/ppermute | solution.py:10
  123.3 20.4 %all-to-all-start = ((bf16[64,8,512]{2,0,1:T(8,128)(2,1)}), bf16[64,8,512]{2,0,1:T(8,128)(2,1)S(1)}, u32[]{:S(2)}, u32[]{:S(2)}) async-start(bf16[64,8,512]{2,0,1:T(8,128)(2,1)} %copy.89), calls=%async_computation | async-start | bytes 1048576 | tf_op jit(solution)/shard_map/all_to_all | solution.py:87
  143.8 10.4 %all-to-all-start.6 = ((bf16[64,8,512]{2,0,1:T(8,128)(2,1)}), bf16[64,8,512]{2,0,1:T(8,128)(2,1)S(1)}, u32[]{:S(2)}, u32[]{:S(2)}) async-start(bf16[64,8,512]{2,0,1:T(8,128)(2,1)} %bitcast.316), calls=%async_computation.6 | async-start | bytes 1048576 | tf_op jit(solution)/shard_map/all_to_all | solution.py:87
  156.6 10.6 %all-to-all-start.1 = ((bf16[8,64,512]{2,1,0:T(8,128)(2,1)}), bf16[8,64,512]{2,1,0:T(8,128)(2,1)S(1)}, u32[]{:S(2)}, u32[]{:S(2)}) async-start(bf16[8,64,512]{2,1,0:T(8,128)(2,1)} %bitcast.24), calls=%async_computation.1 | async-start | bytes 1048576 | tf_op jit(solution)/shard_map/all_to_all | solution.py:90
  167.2 25.1 %all-to-all-start.7 = ((bf16[8,64,512]{2,1,0:T(8,128)(2,1)}), bf16[8,64,512]{2,1,0:T(8,128)(2,1)S(1)}, u32[]{:S(2)}, u32[]{:S(2)}) async-start(bf16[8,64,512]{2,1,0:T(8,128)(2,1)} %bitcast.69), calls=%async_computation.7 | async-start | bytes 1048576 | tf_op jit(solution)/shard_map/all_to_all | solution.py:90
  172.6 114.2 %reduce-scatter.3.cloned.1.call-start = ((), (), s32[]{:S(2)}) async-start(), calls=%async_computation.10 | async-start | bytes 1179648 | tf_op jit(solution)/shard_map/reduce_scatter | solution.py:119
  174.9 37.1 %collective-permute-start.4 = (bf16[64,4096]{1,0:T(8,128)(2,1)}, bf16[64,4096]{1,0:T(8,128)(2,1)}, u32[]{:S(2)}, u32[]{:S(2)}) collective-permute-start(bf16[64,4096]{1,0:T(8,128)(2,1)} %bitcast.115), channel_id=1, source_target_pairs={{0,16},{8,24},{16,32},{24,40},{32,48},{40,56},{48,64},{56,72},{64,... | collective-permute-start | bytes 1572872 | tf_op jit(solution)/shard_map/ppermute | solution.py:10
  174.9 39.9 %collective-permute-start.5 = (bf16[64,4096]{1,0:T(8,128)(2,1)}, bf16[64,4096]{1,0:T(8,128)(2,1)}, u32[]{:S(2)}, u32[]{:S(2)}) collective-permute-start(bf16[64,4096]{1,0:T(8,128)(2,1)} %bitcast.115), channel_id=1, source_target_pairs={{0,8},{8,16},{16,24},{24,32},{32,40},{40,48},{48,56},{56,64},{64,7... | collective-permute-start | bytes 1572872 | tf_op jit(solution)/shard_map/ppermute | solution.py:10
  177.6 47.8 %collective-permute-start.6 = (bf16[64,4096]{1,0:T(8,128)(2,1)}, bf16[64,4096]{1,0:T(8,128)(2,1)}, u32[]{:S(2)}, u32[]{:S(2)}) collective-permute-start(bf16[64,4096]{1,0:T(8,128)(2,1)} %bitcast.115), channel_id=1, source_target_pairs={{0,248},{8,0},{16,8},{24,16},{32,24},{40,32},{48,40},{56,48},{64,5... | collective-permute-start | bytes 1572872 | tf_op jit(solution)/shard_map/ppermute | solution.py:10
  182.5 53.4 %collective-permute-start.7 = (bf16[64,4096]{1,0:T(8,128)(2,1)}, bf16[64,4096]{1,0:T(8,128)(2,1)}, u32[]{:S(2)}, u32[]{:S(2)}) collective-permute-start(bf16[64,4096]{1,0:T(8,128)(2,1)} %bitcast.115), channel_id=1, source_target_pairs={{0,240},{8,248},{16,0},{24,8},{32,16},{40,24},{48,32},{56,40},{64,... | collective-permute-start | bytes 1572872 | tf_op jit(solution)/shard_map/ppermute | solution.py:10
  205.4 126.3 %collective-permute-start.12 = (f32[64,4096]{1,0:T(8,128)}, f32[64,4096]{1,0:T(8,128)}, u32[]{:S(2)}, u32[]{:S(2)}) collective-permute-start(f32[64,4096]{1,0:T(8,128)} %bitcast.311), channel_id=1, source_target_pairs={{0,240},{8,248},{16,0},{24,8},{32,16},{40,24},{48,32},{56,40},{64,... | collective-permute-start | bytes 3145736 | tf_op jit(solution)/shard_map/ppermute | solution.py:10
  250.9 12.7 %all-to-all-start.2 = ((bf16[64,8,512]{2,0,1:T(8,128)(2,1)}), bf16[64,8,512]{2,0,1:T(8,128)(2,1)S(1)}, u32[]{:S(2)}, u32[]{:S(2)}) async-start(bf16[64,8,512]{2,0,1:T(8,128)(2,1)} %copy.102), calls=%async_computation.2 | async-start | bytes 1048576 | tf_op jit(solution)/shard_map/all_to_all | solution.py:87
  256.2 75.4 %reduce-scatter.5.cloned.1.call-start = ((), (), s32[]{:S(2)}) async-start(), calls=%async_computation.11 | async-start | bytes 1179648 | tf_op jit(solution)/shard_map/reduce_scatter | solution.py:120
  261.5 70.2 %collective-permute-start.13 = (f32[64,4096]{1,0:T(8,128)}, f32[64,4096]{1,0:T(8,128)}, u32[]{:S(2)}, u32[]{:S(2)}) collective-permute-start(f32[64,4096]{1,0:T(8,128)} %bitcast.310), channel_id=1, source_target_pairs={{0,248},{8,0},{16,8},{24,16},{32,24},{40,32},{48,40},{56,48},{64,5... | collective-permute-start | bytes 3145736 | tf_op jit(solution)/shard_map/ppermute | solution.py:10
  270.4 61.3 %collective-permute-start.14 = (f32[64,4096]{1,0:T(8,128)}, f32[64,4096]{1,0:T(8,128)}, u32[]{:S(2)}, u32[]{:S(2)}) collective-permute-start(f32[64,4096]{1,0:T(8,128)} %bitcast.309), channel_id=1, source_target_pairs={{0,8},{8,16},{16,24},{24,32},{32,40},{40,48},{48,56},{56,64},{64,7... | collective-permute-start | bytes 3145736 | tf_op jit(solution)/shard_map/ppermute | solution.py:10
  275.7 56.0 %collective-permute-start.15 = (f32[64,4096]{1,0:T(8,128)}, f32[64,4096]{1,0:T(8,128)}, u32[]{:S(2)}, u32[]{:S(2)}) collective-permute-start(f32[64,4096]{1,0:T(8,128)} %bitcast.308), channel_id=1, source_target_pairs={{0,16},{8,24},{16,32},{24,40},{32,48},{40,56},{48,64},{56,72},{64,... | collective-permute-start | bytes 3145736 | tf_op jit(solution)/shard_map/ppermute | solution.py:10
  281.6 54.0 %all-to-all-start.3 = ((bf16[8,64,512]{2,1,0:T(8,128)(2,1)}), bf16[8,64,512]{2,1,0:T(8,128)(2,1)S(1)}, u32[]{:S(2)}, u32[]{:S(2)}) async-start(bf16[8,64,512]{2,1,0:T(8,128)(2,1)} %bitcast.40), calls=%async_computation.3 | async-start | bytes 1048576 | tf_op jit(solution)/shard_map/all_to_all | solution.py:90
  286.8 311.8 %all-reduce.3.cloned.1.call-start = ((), (), s32[]{:S(2)}) async-start(), calls=%async_computation.12 | async-start | bytes 524288 | tf_op jit(solution)/shard_map/psum | solution.py:122
  331.7 270.0 %copy-start.1 = (bf16[512,512]{1,0:T(8,128)(2,1)S(1)}, bf16[512,512]{1,0:T(8,128)(2,1)}, u32[]{:S(2)}) copy-start(bf16[512,512]{1,0:T(8,128)(2,1)} %param.15) | copy-start | bytes 1572868
  (15 other events, 45.5 us)
Sparse Core Ops, SparseCore 0:
  175.9 54.9 reduce-scatter.2
  265.2 66.4 reduce-scatter.4
  334.3 264.2 all-reduce.2
where the time goes:
time: 616 us; the launch traced here: 608 us
  waiting for transfers between devices  333 us (54%)
  matrix products  104 us (17%)
  starting transfers between devices  81.1 us (13%)
  local copies, waits for them, and re-layouts  66.5 us (11%)
  between operations  14.7 us (2%)
  other arithmetic  9.75 us (2%)
    psum x1, waiting for transfers between devices, on_device(): one_grad, two_grad = lax.psum((one_rows, two_rows), 'node')  262 us
    reduce_scatter x1, waiting for transfers between devices, on_device(): lax.psum_scatter(two_part, 'feat', scatter_dimension=0, tiled=True)  44.9 us
    ppermute x16, starting transfers between devices, passed_along(): return lax.ppermute(value, axis, pairs)  40.8 us
    dot_general x10, matrix products, forward_term(): jnp.einsum('hsk,srk->hsr', pieces, tile_set, preferred_element_type=jnp.f...  33.8 us
    dot_general x10, matrix products, forward_term(): jnp.einsum('hsr,bs->hbr', partial_out, selector, precision=lax.Precision....  22.9 us
    dot_general x10, matrix products, backward_term(): jnp.einsum('hsr,srk->hsk', pieces, tile_set, preferred_element_type=jnp.f...  21.2 us
    all_to_all x4, starting transfers between devices, to_features(): lax.all_to_all(field, 'feat', split_axis=0, concat_axis=1, tiled=True)  21 us
    all_to_all x4, starting transfers between devices, to_rows(): lax.all_to_all(field, 'feat', split_axis=1, concat_axis=0, tiled=True)  19.2 us
  transfers between devices with their start and end apart: 27, of which 6 were waited for; matrix products, arithmetic and copies ran while one was open for 27% of the time, Pallas kernels for 0%

commit v1 on v0

v1 whole, which is shorter than its diff:
```python
import functools

import jax
import jax.numpy as jnp
from jax import lax
from jax.experimental import pallas as pl
from jax.experimental.pallas import tpu as pltpu
from jax.sharding import PartitionSpec as P

GROUP = 8
VMEM = pl.BlockSpec(memory_space=pltpu.VMEM)
SMEM = pl.BlockSpec(memory_space=pltpu.SMEM)
ANY = pl.BlockSpec(memory_space=pl.ANY)


def load_tiles(tiles_ref, buf, sems, slots, offsets):
    return [
        pltpu.make_async_copy(
            tiles_ref.at[pl.ds(o * slots, slots)],
            buf.at[pl.ds(o * slots, slots)],
            sems.at[o],
        )
        for o in range(offsets)
    ]


def accumulate(o, slots, counts, take, give, source, buf, target, block, spare, transposed):
    count = counts[o]
    contract = (((1,), (1,)), ((), ())) if transposed else (((1,), (0,)), ((), ()))

    def step(g, carry):
        parts = []
        for i in range(GROUP):
            s = g * GROUP + i
            t = o * slots + s
            c = pl.multiple_of(take[t] * block, block)
            product = lax.dot_general(
                source[:, pl.ds(c, block)],
                buf[t],
                contract,
                preferred_element_type=jnp.float32,
            )
            r = jnp.where(s < count, give[t], spare)
            parts.append((pl.multiple_of(r * block, block), product))
        for r, product in parts:
            target[:, pl.ds(r, block)] += product
        return carry

    lax.fori_loop(0, (count + GROUP - 1) // GROUP, step, 0)


def forward_kernel(slots, block, rows, cols, counts, *refs):
    offsets = counts.shape[0]
    panels = refs[:offsets]
    tiles_ref, out_ref, buf, acc, sems = refs[offsets:]
    width = out_ref.shape[1]
    copies = load_tiles(tiles_ref, buf, sems, slots, offsets)
    for copy in copies:
        copy.start()
    acc[...] = jnp.zeros_like(acc)
    for o in range(offsets):
        copies[o].wait()
        accumulate(
            o, slots, counts, cols, rows, panels[o], buf, acc, block, width // block, True
        )
    out_ref[...] = acc[:, :width].astype(out_ref.dtype)


def backward_kernel(slots, block, rows, cols, counts, panel, tiles_ref, *refs):
    offsets = counts.shape[0]
    outs = refs[:offsets]
    buf, acc, sems = refs[offsets:]
    width = panel.shape[1]
    copies = load_tiles(tiles_ref, buf, sems, slots, offsets)
    for copy in copies:
        copy.start()
    for o in range(offsets):
        acc[...] = jnp.zeros_like(acc)
        copies[o].wait()
        accumulate(
            o, slots, counts, rows, cols, panel, buf, acc, block, width // block, False
        )
        outs[o][...] = acc[:, :width].astype(outs[o].dtype)


def dense_kernel(agg, spread, one, two, one_t, two_t, out, back, one_grad, two_grad):
    f32 = functools.partial(jnp.dot, preferred_element_type=jnp.float32)
    tail = (((1,), (1,)), ((), ()))
    pre = f32(one_t[...], agg[...])
    sigma = 1.0 / (1.0 + jnp.exp(-pre))
    act = (pre * sigma).astype(jnp.bfloat16)
    out[...] = f32(two_t[...], act).astype(jnp.bfloat16)
    two_grad[...] = lax.dot_general(
        act, spread[...], tail, preferred_element_type=jnp.float32
    ).astype(two_grad.dtype)
    act_back = f32(two[...], spread[...]).astype(jnp.bfloat16).astype(jnp.float32)
    pre_back = (act_back * sigma * (1.0 + pre * (1.0 - sigma))).astype(jnp.bfloat16)
    back[...] = f32(one[...], pre_back).astype(jnp.bfloat16)
    one_grad[...] = lax.dot_general(
        agg[...], pre_back, tail, preferred_element_type=jnp.float32
    ).astype(one_grad.dtype)


def passed_along(value, axis, steps):
    count = lax.axis_size(axis)
    pairs = [(source, (source + steps) % count) for source in range(count)]
    return lax.ppermute(value, axis, pairs)


def on_device(features, tiles, tile_rows, tile_cols, counts, weight_one, weight_two, cotangent):
    offsets = counts.shape[0]
    reach = (offsets - 1) // 2
    slots = tile_rows.shape[0] // offsets
    block = tiles.shape[-1]
    height, width = features.shape
    depth = weight_one.shape[0]
    share = width // lax.axis_size("feat")
    limit = pltpu.CompilerParams(vmem_limit_bytes=48 << 20)
    bf16, f32 = jnp.bfloat16, jnp.float32
    scratch = [
        pltpu.VMEM(tiles.shape, tiles.dtype),
        pltpu.VMEM((height, width + block), f32),
        pltpu.SemaphoreType.DMA((offsets,)),
    ]
    cost = pl.CostEstimate(
        flops=2 * tiles.size * height, bytes_accessed=tiles.size * 2, transcendentals=0
    )

    def forward(panel):
        panels = [
            panel if o == reach else passed_along(panel, "node", reach - o)
            for o in range(offsets)
        ]
        return pl.pallas_call(
            functools.partial(forward_kernel, slots, block),
            out_shape=jax.ShapeDtypeStruct((height, width), bf16),
            in_specs=[SMEM] * 3 + [VMEM] * offsets + [ANY],
            out_specs=VMEM,
            scratch_shapes=scratch,
            compiler_params=limit,
            cost_estimate=cost,
        )(tile_rows, tile_cols, counts, *panels, tiles)

    def backward(panel):
        parts = pl.pallas_call(
            functools.partial(backward_kernel, slots, block),
            out_shape=[
                jax.ShapeDtypeStruct((height, width), f32 if o == reach else bf16)
                for o in range(offsets)
            ],
            in_specs=[SMEM] * 3 + [VMEM, ANY],
            out_specs=[VMEM] * offsets,
            scratch_shapes=scratch,
            compiler_params=limit,
            cost_estimate=cost,
        )(tile_rows, tile_cols, counts, panel, tiles)
        total = parts[reach]
        for o in range(offsets):
            if o != reach:
                total = total + passed_along(parts[o], "node", o - reach).astype(f32)
        return total.astype(bf16)

    def to_rows(field):
        return lax.all_to_all(field, "feat", split_axis=1, concat_axis=0, tiled=True)

    def to_features(field):
        return lax.all_to_all(field, "feat", split_axis=0, concat_axis=1, tiled=True)

    agg = to_rows(forward(features))
    spread = to_rows(backward(cotangent))
    out, back, one_part, two_part = pl.pallas_call(
        dense_kernel,
        out_shape=[jax.ShapeDtypeStruct((depth, share), bf16)] * 2
        + [jax.ShapeDtypeStruct((depth, depth), bf16)] * 2,
        in_specs=[VMEM] * 6,
        out_specs=[VMEM] * 4,
        compiler_params=limit,
    )(agg, spread, weight_one, weight_two, weight_one.T, weight_two.T)
    layer_out = forward(to_features(out))
    feature_grad = backward(to_features(back))

    grads = jnp.stack([one_part, two_part])
    feats, nodes = lax.axis_size("feat"), lax.axis_size("node")
    grads = lax.all_to_all(
        grads.reshape(2, feats, depth // feats, depth), "feat", split_axis=1, concat_axis=1
    )
    grads = jnp.sum(grads.astype(f32), axis=1)
    grads = lax.all_to_all(
        grads.reshape(nodes, -1, depth), "node", split_axis=0, concat_axis=0
    )
    grads = jnp.sum(grads, axis=0)
    grads = lax.all_gather(grads, "node", axis=0).reshape(2, depth // feats, depth)
    return (layer_out, feature_grad, grads[0], grads[1])


def solution(mesh):
    in_specs = (
        P("feat", "node"),
        P("node", None, None),
        P("node"),
        P("node"),
        P("node"),
        P(),
        P(),
        P("feat", "node"),
    )
    out_specs = (P("feat", "node"), P("feat", "node"), P("feat", None), P("feat", None))
    return jax.shard_map(
        on_device, mesh=mesh, in_specs=in_specs, out_specs=out_specs, check_vma=False
    )
```

time: 616 us -> 225 us (0.37)
  waiting for transfers between devices: 333 us -> 44.5 us
  matrix products: 104 us -> 0 us
  local copies, waits for them, and re-layouts: 66.5 us -> 8.25 us
  blocking collectives: 0 us -> 49.8 us
  Pallas kernels: 0 us -> 30.2 us
  between operations: 14.7 us -> 0.84 us
    psum x1 -> x0, waiting for transfers between devices: 262 us -> none  [on_device(): one_grad, two_grad = lax.psum((one_rows, two_rows), 'node')]
    dot_general x46 -> x0, matrix products: 104 us -> none  [the longest x10 33.8 us: forward_term(): jnp.einsum('hsk,srk->hsr', pieces, tile_set, preferred_element_type=jnp.f...]
    reduce_scatter x2 -> x0, waiting for transfers between devices: 44.9 us -> none  [the longest x1 44.9 us: on_device(): lax.psum_scatter(two_part, 'feat', scatter_dimension=0, tiled=True)]
    all_gather x0 -> x1, blocking collectives: none -> 37.4 us  [on_device(): lax.all_gather(grads, 'node', axis=0).reshape(2, depth // feats, depth)]
    all_to_all x0 -> x2, starting transfers between devices: none -> 33.9 us  [the longest x1 28.2 us: on_device(): lax.all_to_all(grads.reshape(nodes, -1, depth), 'node', split_axis=0, con...]
    pallas_call x0 -> x5, Pallas kernels: none -> 30.2 us  [the longest x2 14.2 us: forward(): pl.pallas_call(functools.partial(forward_kernel, slots, block), out_shape...]
    gather x20 -> x0, local copies, waits for them, and re-layouts: 28.1 us -> none  [the longest x10 14.1 us: backward_term(): jnp.take(panel.reshape(width, blocks_count, block), slot_rows, axis=1)]
    ppermute x16, waiting for transfers between devices: 6.37 us -> 33.2 us  [passed_along(): return lax.ppermute(value, axis, pairs)]
  transfers between devices with their start and end apart: 27 -> 21, of which waited for: 6 -> 9; matrix products, arithmetic and copies ran while one was open for 27% -> 5% of each run, Pallas kernels for 0% -> 13%
where the time goes in v1:
time: 225 us; the launch traced here: 223 us
  starting transfers between devices  81.7 us (36%)
  blocking collectives  49.8 us (22%)
  waiting for transfers between devices  44.5 us (20%)
  Pallas kernels  30.2 us (13%)
  local copies, waits for them, and re-layouts  8.25 us (4%)
  other arithmetic  8.2 us (4%)
    all_gather x1, blocking collectives, on_device(): lax.all_gather(grads, 'node', axis=0).reshape(2, depth // feats, depth)  37.4 us
    ppermute x16, starting transfers between devices, passed_along(): return lax.ppermute(value, axis, pairs)  34.2 us
    ppermute x16, waiting for transfers between devices, passed_along(): return lax.ppermute(value, axis, pairs)  33.2 us
    all_to_all x1, starting transfers between devices, on_device(): lax.all_to_all(grads.reshape(nodes, -1, depth), 'node', split_axis=0, con...  28.2 us
    pallas_call x2, Pallas kernels, forward(): pl.pallas_call(functools.partial(forward_kernel, slots, block), out_shape...  14.2 us
    pallas_call x2, Pallas kernels, backward(): pl.pallas_call(functools.partial(backward_kernel, slots, block), out_shap...  13.9 us
    all_to_all x1, blocking collectives, to_features(): lax.all_to_all(field, 'feat', split_axis=0, concat_axis=1, tiled=True)  12.4 us
    all_to_all x2, starting transfers between devices, to_rows(): lax.all_to_all(field, 'feat', split_axis=1, concat_axis=0, tiled=True)  8.55 us
  transfers between devices with their start and end apart: 21, of which 9 were waited for; matrix products, arithmetic and copies ran while one was open for 5% of the time, Pallas kernels for 13%

profile of v1, /device:TPU:25, one launch (start us, length us, event | category | flops | bytes accessed | tf_op | source)
XLA Modules:
  0.0 223.5 jit_solution(14277306104045895431)
XLA Ops:
  1.4 1.6 collective-permute-start.1
  3.0 1.6 collective-permute-start
  4.6 9.5 %collective-permute-start.3 = (bf16[64,4096]{1,0:T(8,128)(2,1)}, bf16[64,4096]{1,0:T(8,128)(2,1)S(1)}, u32[]{:S(2)}, u32[]{:S(2)}) collective-permute-start(bf16[64,4096]{1,0:T(8,128)(2,1)} %refs_2_.1), channel_id=1, source_target_pairs={{0,240},{8,248},{16,0},{24,8},{32,16},{40,24},{48,32},{56,40},{64,... | collective-permute-start | bytes 1572872 | tf_op jit(solution)/shard_map/ppermute | solution.py:107
  17.2 7.0 %shard_map.112 = (bf16[64,4096]{1,0:T(8,128)(2,1)}, bf16[64,4096]{1,0:T(8,128)(2,1)}, f32[64,4096]{1,0:T(8,128)S(1)}, bf16[64,4096]{1,0:T(8,128)(2,1)}, bf16[64,4096]{1,0:T(8,128)(2,1)S(1)}) custom-call(s32[240]{0:T(256)S(1)} %copy-done.7, s32[240]{0:T(256)S(1)} %copy-done.9, s32[5]{0:T(128)S(1)} %copy-done.11, bf16[64,4096]{1,0:T(8,128)(2,1)S(1)} %copy-done.2, ...), custom_call_target="tpu_custom_call" | custom-call | flops 503316480 | bytes 7864320 | tf_op jit(solution)/shard_map/pallas_call | solution.py:145
  24.2 3.6 %collective-permute-start.4 = (bf16[64,4096]{1,0:T(8,128)(2,1)}, bf16[64,4096]{1,0:T(8,128)(2,1)}, u32[]{:S(2)}, u32[]{:S(2)}) collective-permute-start(bf16[64,4096]{1,0:T(8,128)(2,1)} %get-tuple-element.19), channel_id=1, source_target_pairs={{0,240},{8,248},{16,0},{24,8},{32,16},{40,24},{48,32},{56,40},{64,... | collective-permute-start | bytes 1572872 | tf_op jit(solution)/shard_map/ppermute | solution.py:107
  27.9 1.7 collective-permute-start.6
  29.6 2.5 %collective-permute-done.refs_0_ = bf16[64,4096]{1,0:T(8,128)(2,1)S(1)} collective-permute-done((bf16[64,4096]{1,0:T(8,128)(2,1)}, bf16[64,4096]{1,0:T(8,128)(2,1)S(1)}, u32[]{:S(2)}, u32[]{:S(2)}) %collective-permute-start) | collective-permute-done | bytes 524320 | tf_op jit(solution)/shard_map/ppermute | solution.py:107
  32.1 6.7 %shard_map.111 = bf16[64,4096]{1,0:T(8,128)(2,1)S(1)} custom-call(s32[240]{0:T(256)S(1)} %copy-done.7, s32[240]{0:T(256)S(1)} %copy-done.9, s32[5]{0:T(128)S(1)} %copy-done.11, bf16[64,4096]{1,0:T(8,128)(2,1)S(1)} %collective-permute-done.refs_0_, bf16[64,4096]{1,0:T(8,128)(2,1)S(1)} %collective-permute-done.1.refs_1_, bf16[64,4096]{1,0:T(8,128)(2,1)S(1)} %copy-done.3, ...), custom_call_target="tpu_custom_call" | custom-call | flops 503316480 | bytes 7864320 | tf_op jit(solution)/shard_map/pallas_call | solution.py:134
  39.7 4.2 %all-to-all-start = ((bf16[64,8,512]{2,0,1:T(8,128)(2,1)}), bf16[64,8,512]{2,0,1:T(8,128)(2,1)S(1)}, u32[]{:S(2)}, u32[]{:S(2)}) async-start(bf16[64,8,512]{2,0,1:T(8,128)(2,1)} %bitcast.48), calls=%async_computation | async-start | bytes 1048576 | tf_op jit(solution)/shard_map/all_to_all | solution.py:164
  44.2 7.4 %collective-permute-done.7 = bf16[64,4096]{1,0:T(8,128)(2,1)} collective-permute-done((bf16[64,4096]{1,0:T(8,128)(2,1)S(1)}, bf16[64,4096]{1,0:T(8,128)(2,1)}, u32[]{:S(2)}, u32[]{:S(2)}) %collective-permute-start.7) | collective-permute-done | bytes 524320 | tf_op jit(solution)/shard_map/ppermute | solution.py:107
  51.5 1.8 add_convert_fusion.1
  55.2 4.4 %all-to-all-start.1 = ((bf16[64,8,512]{2,0,1:T(8,128)(2,1)}), bf16[64,8,512]{2,0,1:T(8,128)(2,1)S(1)}, u32[]{:S(2)}, u32[]{:S(2)}) async-start(bf16[64,8,512]{2,0,1:T(8,128)(2,1)} %bitcast.29), calls=%async_computation.1 | async-start | bytes 1048576 | tf_op jit(solution)/shard_map/all_to_all | solution.py:164
  60.1 7.0 %all-to-all-done.1 = bf16[64,8,512]{2,0,1:T(8,128)(2,1)S(1)} async-done(((bf16[64,8,512]{2,0,1:T(8,128)(2,1)}), bf16[64,8,512]{2,0,1:T(8,128)(2,1)S(1)}, u32[]{:S(2)}, u32[]{:S(2)}) %all-to-all-start.1) | async-done | bytes 524320 | tf_op jit(solution)/shard_map/all_to_all | solution.py:164
  67.1 2.1 shard_map.113
  70.0 12.4 %all_to_all.86 = bf16[8,64,512]{2,1,0:T(8,128)(2,1)S(1)} all-to-all(bf16[8,64,512]{2,1,0:T(8,128)(2,1)S(1)} %bitcast.43), channel_id=1, replica_groups=mesh['node'=32,'feat'=8] {'feat'}, dimensions={0} | all-to-all | bytes 1048576 | tf_op jit(solution)/shard_map/all_to_all | solution.py:167
  82.4 5.1 %all-to-all-start.2 = ((bf16[8,64,512]{2,1,0:T(8,128)(2,1)}), bf16[8,64,512]{2,1,0:T(8,128)(2,1)S(1)}, u32[]{:S(2)}, u32[]{:S(2)}) async-start(bf16[8,64,512]{2,1,0:T(8,128)(2,1)} %bitcast.42), calls=%async_computation.2 | async-start | bytes 1048576 | tf_op jit(solution)/shard_map/all_to_all | solution.py:167
  87.5 2.3 %pad_maximum_fusion = bf16[2,8,64,512]{3,2,0,1:T(8,128)(2,1)} fusion(bf16[1,8,64,512]{3,2,0,1:T(8,128)(2,1)} %bitcast.45, bf16[1,8,64,512]{3,2,0,1:T(8,128)(2,1)} %bitcast.44), kind=kLoop, calls=%fused_computation.1 | loop fusion | flops 524288 | bytes 2097152 | tf_op jit(solution)/shard_map/stack | solution.py:182
  89.7 3.3 %all-to-all-done.2 = bf16[8,64,512]{2,1,0:T(8,128)(2,1)S(1)} async-done(((bf16[8,64,512]{2,1,0:T(8,128)(2,1)}), bf16[8,64,512]{2,1,0:T(8,128)(2,1)S(1)}, u32[]{:S(2)}, u32[]{:S(2)}) %all-to-all-start.2) | async-done | bytes 524320 | tf_op jit(solution)/shard_map/all_to_all | solution.py:167
  93.0 5.7 %all-to-all-start.4 = ((bf16[2,8,64,512]{3,2,0,1:T(8,128)(2,1)}), bf16[2,8,64,512]{3,2,0,1:T(8,128)(2,1)}, u32[]{:S(2)}, u32[]{:S(2)}) async-start(bf16[2,8,64,512]{3,2,0,1:T(8,128)(2,1)} %pad_maximum_fusion), calls=%async_computation.4 | async-start | bytes 2097152 | tf_op jit(solution)/shard_map/all_to_all | solution.py:184
  98.8 6.9 %shard_map.115 = (bf16[64,4096]{1,0:T(8,128)(2,1)}, bf16[64,4096]{1,0:T(8,128)(2,1)}, f32[64,4096]{1,0:T(8,128)S(1)}, bf16[64,4096]{1,0:T(8,128)(2,1)S(1)}, bf16[64,4096]{1,0:T(8,128)(2,1)S(1)}) custom-call(s32[240]{0:T(256)S(1)} %copy-done.8, s32[240]{0:T(256)S(1)} %copy-done.10, s32[5]{0:T(128)S(1)} %copy-done.12, bf16[64,4096]{1,0:T(8,128)(2,1)S(1)} %bitcast.36, ...), custom_call_target="tpu_custom_call" | custom-call | flops 503316480 | bytes 7864320 | tf_op jit(solution)/shard_map/pallas_call | solution.py:145
  105.7 5.2 %collective-permute-start.12 = (bf16[64,4096]{1,0:T(8,128)(2,1)}, bf16[64,4096]{1,0:T(8,128)(2,1)}, u32[]{:S(2)}, u32[]{:S(2)}) collective-permute-start(bf16[64,4096]{1,0:T(8,128)(2,1)} %get-tuple-element.26), channel_id=1, source_target_pairs={{0,240},{8,248},{16,0},{24,8},{32,16},{40,24},{48,32},{56,40},{64,... | collective-permute-start | bytes 1572872 | tf_op jit(solution)/shard_map/ppermute | solution.py:107
  111.0 1.6 collective-permute-start.14
  112.7 5.2 %collective-permute-start.11 = (bf16[64,4096]{1,0:T(8,128)(2,1)S(1)}, bf16[64,4096]{1,0:T(8,128)(2,1)S(1)}, u32[]{:S(2)}, u32[]{:S(2)}) collective-permute-start(bf16[64,4096]{1,0:T(8,128)(2,1)S(1)} %bitcast.31), channel_id=1, source_target_pairs={{0,240},{8,248},{16,0},{24,8},{32,16},{40,24},{48,32},{56,40},{64,... | collective-permute-start | bytes 1572872 | tf_op jit(solution)/shard_map/ppermute | solution.py:107
  117.8 1.4 convert_reduce_fusion
  120.0 28.2 %all-to-all-start.5 = ((f32[32,4,512]{2,1,0:T(4,128)}), f32[32,4,512]{2,1,0:T(4,128)S(1)}, u32[]{:S(2)}, u32[]{:S(2)}) async-start(f32[32,4,512]{2,1,0:T(4,128)} %reshape.33), calls=%async_computation.5 | async-start | bytes 524288 | tf_op jit(solution)/shard_map/all_to_all | solution.py:188
  148.5 1.5 collective-permute-start.9
  151.4 2.6 %add_convert_fusion = bf16[64,4096]{1,0:T(8,128)(2,1)} fusion(bf16[64,4096]{1,0:T(8,128)(2,1)} %collective-permute-done.15, bf16[64,4096]{1,0:T(8,128)(2,1)} %collective-permute-done.14, bf16[64,4096]{1,0:T(8,128)(2,1)} %collective-permute-done.13, f32[64,4096]{1,0:T(8,128)S(1)} %get-tuple-element.25, bf16[64,4096]{1,0:T(8,128)(2,1)} %collective-permute-done.12), kind=kLoop, calls=%fused_computation.2 | loop fusion | flops 2359296 | bytes 3670016 | tf_op jit(solution)/shard_map/convert_element_type | solution.py:161
  154.0 8.1 %collective-permute-done.10.refs_3_ = bf16[64,4096]{1,0:T(8,128)(2,1)S(1)} collective-permute-done((bf16[64,4096]{1,0:T(8,128)(2,1)S(1)}, bf16[64,4096]{1,0:T(8,128)(2,1)S(1)}, u32[]{:S(2)}, u32[]{:S(2)}) %collective-permute-start.10) | collective-permute-done | bytes 524320 | tf_op jit(solution)/shard_map/ppermute | solution.py:107
  162.1 2.5 %collective-permute-done.9.refs_1_ = bf16[64,4096]{1,0:T(8,128)(2,1)S(1)} collective-permute-done((bf16[64,4096]{1,0:T(8,128)(2,1)S(1)}, bf16[64,4096]{1,0:T(8,128)(2,1)S(1)}, u32[]{:S(2)}, u32[]{:S(2)}) %collective-permute-start.9) | collective-permute-done | bytes 524320 | tf_op jit(solution)/shard_map/ppermute | solution.py:107
  164.6 12.4 %collective-permute-done.8.refs_0_ = bf16[64,4096]{1,0:T(8,128)(2,1)S(1)} collective-permute-done((bf16[64,4096]{1,0:T(8,128)(2,1)S(1)}, bf16[64,4096]{1,0:T(8,128)(2,1)S(1)}, u32[]{:S(2)}, u32[]{:S(2)}) %collective-permute-start.8) | collective-permute-done | bytes 524320 | tf_op jit(solution)/shard_map/ppermute | solution.py:107
  177.1 7.5 %shard_map.114 = bf16[64,4096]{1,0:T(8,128)(2,1)} custom-call(s32[240]{0:T(256)S(1)} %copy-done.8, s32[240]{0:T(256)S(1)} %copy-done.10, s32[5]{0:T(128)S(1)} %copy-done.12, bf16[64,4096]{1,0:T(8,128)(2,1)S(1)} %collective-permute-done.8.refs_0_, bf16[64,4096]{1,0:T(8,128)(2,1)S(1)} %collective-permute-done.9.refs_1_, bf16[64,4096]{1,0:T(8,128)(2,1)S(1)} %bitcast.35, ...), custom_call_target="tpu_custom_call" | custom-call | flops 503316480 | bytes 7864320 | tf_op jit(solution)/shard_map/pallas_call | solution.py:134
  184.6 37.4 %all-gather.1 = f32[32,4,512]{2,1,0:T(4,128)S(1)} all-gather(f32[1,4,512]{2,1,0:T(4,128)S(1)} %bitcast.50), channel_id=2, replica_groups=mesh['node'=32,'feat'=8] {'node'}, dimensions={0}, use_global_device_ids=true | all-gather | bytes 270336 | tf_op jit(solution)/shard_map/all_gather | solution.py:192
  (58 shorter events, 12.2 us)
Async XLA Ops:
  0.6 27.2 %collective-permute-start.2 = (bf16[64,4096]{1,0:T(8,128)(2,1)}, bf16[64,4096]{1,0:T(8,128)(2,1)S(1)}, u32[]{:S(2)}, u32[]{:S(2)}) collective-permute-start(bf16[64,4096]{1,0:T(8,128)(2,1)} %refs_2_.1), channel_id=1, source_target_pairs={{0,248},{8,0},{16,8},{24,16},{32,24},{40,32},{48,40},{56,48},{64,5... | collective-permute-start | bytes 1572872 | tf_op jit(solution)/shard_map/ppermute | solution.py:107
  1.4 26.5 %collective-permute-start.1 = (bf16[64,4096]{1,0:T(8,128)(2,1)}, bf16[64,4096]{1,0:T(8,128)(2,1)S(1)}, u32[]{:S(2)}, u32[]{:S(2)}) collective-permute-start(bf16[64,4096]{1,0:T(8,128)(2,1)} %refs_2_.1), channel_id=1, source_target_pairs={{0,8},{8,16},{16,24},{24,32},{32,40},{40,48},{48,56},{56,64},{64,7... | collective-permute-start | bytes 1572872 | tf_op jit(solution)/shard_map/ppermute | solution.py:107
  3.0 29.1 %collective-permute-start = (bf16[64,4096]{1,0:T(8,128)(2,1)}, bf16[64,4096]{1,0:T(8,128)(2,1)S(1)}, u32[]{:S(2)}, u32[]{:S(2)}) collective-permute-start(bf16[64,4096]{1,0:T(8,128)(2,1)} %refs_2_.1), channel_id=1, source_target_pairs={{0,16},{8,24},{16,32},{24,40},{32,48},{40,56},{48,64},{56,72},{64,... | collective-permute-start | bytes 1572872 | tf_op jit(solution)/shard_map/ppermute | solution.py:107
  4.6 27.5 %collective-permute-start.3 = (bf16[64,4096]{1,0:T(8,128)(2,1)}, bf16[64,4096]{1,0:T(8,128)(2,1)S(1)}, u32[]{:S(2)}, u32[]{:S(2)}) collective-permute-start(bf16[64,4096]{1,0:T(8,128)(2,1)} %refs_2_.1), channel_id=1, source_target_pairs={{0,240},{8,248},{16,0},{24,8},{32,16},{40,24},{48,32},{56,40},{64,... | collective-permute-start | bytes 1572872 | tf_op jit(solution)/shard_map/ppermute | solution.py:107
  14.1 1.0 copy-start.2
  15.8 0.7 copy-start.9
  17.2 15.0 %copy-start.3 = (bf16[64,4096]{1,0:T(8,128)(2,1)S(1)}, bf16[64,4096]{1,0:T(8,128)(2,1)}, u32[]{:S(2)}) copy-start(bf16[64,4096]{1,0:T(8,128)(2,1)} %refs_2_.1) | copy-start | bytes 1572868
  24.2 19.6 %collective-permute-start.4 = (bf16[64,4096]{1,0:T(8,128)(2,1)}, bf16[64,4096]{1,0:T(8,128)(2,1)}, u32[]{:S(2)}, u32[]{:S(2)}) collective-permute-start(bf16[64,4096]{1,0:T(8,128)(2,1)} %get-tuple-element.19), channel_id=1, source_target_pairs={{0,240},{8,248},{16,0},{24,8},{32,16},{40,24},{48,32},{56,40},{64,... | collective-permute-start | bytes 1572872 | tf_op jit(solution)/shard_map/ppermute | solution.py:107
  27.8 16.3 %collective-permute-start.5 = (bf16[64,4096]{1,0:T(8,128)(2,1)}, bf16[64,4096]{1,0:T(8,128)(2,1)}, u32[]{:S(2)}, u32[]{:S(2)}) collective-permute-start(bf16[64,4096]{1,0:T(8,128)(2,1)} %get-tuple-element.20), channel_id=1, source_target_pairs={{0,248},{8,0},{16,8},{24,16},{32,24},{40,32},{48,40},{56,48},{64,5... | collective-permute-start | bytes 1572872 | tf_op jit(solution)/shard_map/ppermute | solution.py:107
  27.9 16.3 %collective-permute-start.6 = (bf16[64,4096]{1,0:T(8,128)(2,1)}, bf16[64,4096]{1,0:T(8,128)(2,1)}, u32[]{:S(2)}, u32[]{:S(2)}) collective-permute-start(bf16[64,4096]{1,0:T(8,128)(2,1)} %get-tuple-element.21), channel_id=1, source_target_pairs={{0,8},{8,16},{16,24},{24,32},{32,40},{40,48},{48,56},{56,64},{64,7... | collective-permute-start | bytes 1572872 | tf_op jit(solution)/shard_map/ppermute | solution.py:107
  32.1 27.5 %copy-start = (bf16[512,512]{1,0:T(8,128)(2,1)S(1)}, bf16[512,512]{1,0:T(8,128)(2,1)}, u32[]{:S(2)}) copy-start(bf16[512,512]{1,0:T(8,128)(2,1)} %one.1) | copy-start | bytes 1572868
  32.1 27.7 %copy-start.1 = (bf16[512,512]{1,0:T(8,128)(2,1)S(1)}, bf16[512,512]{1,0:T(8,128)(2,1)}, u32[]{:S(2)}) copy-start(bf16[512,512]{1,0:T(8,128)(2,1)} %two.1) | copy-start | bytes 1572868
  32.1 19.4 %collective-permute-start.7 = (bf16[64,4096]{1,0:T(8,128)(2,1)S(1)}, bf16[64,4096]{1,0:T(8,128)(2,1)}, u32[]{:S(2)}, u32[]{:S(2)}) collective-permute-start(bf16[64,4096]{1,0:T(8,128)(2,1)S(1)} %get-tuple-element.22), channel_id=1, source_target_pairs={{0,16},{8,24},{16,32},{24,40},{32,48},{40,56},{48,64},{56,72},{64,... | collective-permute-start | bytes 1572872 | tf_op jit(solution)/shard_map/ppermute | solution.py:107
  39.7 15.5 %all-to-all-start = ((bf16[64,8,512]{2,0,1:T(8,128)(2,1)}), bf16[64,8,512]{2,0,1:T(8,128)(2,1)S(1)}, u32[]{:S(2)}, u32[]{:S(2)}) async-start(bf16[64,8,512]{2,0,1:T(8,128)(2,1)} %bitcast.48), calls=%async_computation | async-start | bytes 1048576 | tf_op jit(solution)/shard_map/all_to_all | solution.py:164
  53.4 45.4 %copy-start.8 = (s32[240]{0:T(256)S(1)}, s32[240]{0:T(256)}, u32[]{:S(2)}) copy-start(s32[240]{0:T(256)} %rows.7) | copy-start | bytes 2884
  53.4 45.4 %copy-start.10 = (s32[240]{0:T(256)S(1)}, s32[240]{0:T(256)}, u32[]{:S(2)}) copy-start(s32[240]{0:T(256)} %cols.7) | copy-start | bytes 2884
  53.4 45.4 %copy-start.12 = (s32[5]{0:T(128)S(1)}, s32[5]{0:T(128)}, u32[]{:S(2)}) copy-start(s32[5]{0:T(128)} %counts.7) | copy-start | bytes 64
  55.2 11.8 %all-to-all-start.1 = ((bf16[64,8,512]{2,0,1:T(8,128)(2,1)}), bf16[64,8,512]{2,0,1:T(8,128)(2,1)S(1)}, u32[]{:S(2)}, u32[]{:S(2)}) async-start(bf16[64,8,512]{2,0,1:T(8,128)(2,1)} %bitcast.29), calls=%async_computation.1 | async-start | bytes 1048576 | tf_op jit(solution)/shard_map/all_to_all | solution.py:164
  69.2 0.8 copy-start.6
  70.0 12.4 %copy-start.5 = (bf16[512,512]{1,0:T(8,128)(2,1)}, bf16[512,512]{1,0:T(8,128)(2,1)S(1)}, u32[]{:S(2)}) copy-start(bf16[512,512]{1,0:T(8,128)(2,1)S(1)} %get-tuple-element.30) | copy-start | bytes 1572868
  70.0 12.4 %copy-start.4 = (bf16[512,512]{1,0:T(8,128)(2,1)}, bf16[512,512]{1,0:T(8,128)(2,1)S(1)}, u32[]{:S(2)}) copy-start(bf16[512,512]{1,0:T(8,128)(2,1)S(1)} %get-tuple-element.23) | copy-start | bytes 1572868
  82.4 10.6 %all-to-all-start.2 = ((bf16[8,64,512]{2,1,0:T(8,128)(2,1)}), bf16[8,64,512]{2,1,0:T(8,128)(2,1)S(1)}, u32[]{:S(2)}, u32[]{:S(2)}) async-start(bf16[8,64,512]{2,1,0:T(8,128)(2,1)} %bitcast.42), calls=%async_computation.2 | async-start | bytes 1048576 | tf_op jit(solution)/shard_map/all_to_all | solution.py:167
  93.0 24.8 %all-to-all-start.4 = ((bf16[2,8,64,512]{3,2,0,1:T(8,128)(2,1)}), bf16[2,8,64,512]{3,2,0,1:T(8,128)(2,1)}, u32[]{:S(2)}, u32[]{:S(2)}) async-start(bf16[2,8,64,512]{3,2,0,1:T(8,128)(2,1)} %pad_maximum_fusion), calls=%async_computation.4 | async-start | bytes 2097152 | tf_op jit(solution)/shard_map/all_to_all | solution.py:184
  105.7 42.5 %collective-permute-start.12 = (bf16[64,4096]{1,0:T(8,128)(2,1)}, bf16[64,4096]{1,0:T(8,128)(2,1)}, u32[]{:S(2)}, u32[]{:S(2)}) collective-permute-start(bf16[64,4096]{1,0:T(8,128)(2,1)} %get-tuple-element.26), channel_id=1, source_target_pairs={{0,240},{8,248},{16,0},{24,8},{32,16},{40,24},{48,32},{56,40},{64,... | collective-permute-start | bytes 1572872 | tf_op jit(solution)/shard_map/ppermute | solution.py:107
  110.9 37.6 %collective-permute-start.13 = (bf16[64,4096]{1,0:T(8,128)(2,1)}, bf16[64,4096]{1,0:T(8,128)(2,1)}, u32[]{:S(2)}, u32[]{:S(2)}) collective-permute-start(bf16[64,4096]{1,0:T(8,128)(2,1)} %get-tuple-element.27), channel_id=1, source_target_pairs={{0,248},{8,0},{16,8},{24,16},{32,24},{40,32},{48,40},{56,48},{64,5... | collective-permute-start | bytes 1572872 | tf_op jit(solution)/shard_map/ppermute | solution.py:107
  111.0 39.0 %collective-permute-start.14 = (bf16[64,4096]{1,0:T(8,128)(2,1)S(1)}, bf16[64,4096]{1,0:T(8,128)(2,1)}, u32[]{:S(2)}, u32[]{:S(2)}) collective-permute-start(bf16[64,4096]{1,0:T(8,128)(2,1)S(1)} %get-tuple-element.28), channel_id=1, source_target_pairs={{0,8},{8,16},{16,24},{24,32},{32,40},{40,48},{48,56},{56,64},{64,7... | collective-permute-start | bytes 1572872 | tf_op jit(solution)/shard_map/ppermute | solution.py:107
  112.6 38.8 %collective-permute-start.15 = (bf16[64,4096]{1,0:T(8,128)(2,1)S(1)}, bf16[64,4096]{1,0:T(8,128)(2,1)}, u32[]{:S(2)}, u32[]{:S(2)}) collective-permute-start(bf16[64,4096]{1,0:T(8,128)(2,1)S(1)} %get-tuple-element.29), channel_id=1, source_target_pairs={{0,16},{8,24},{16,32},{24,40},{32,48},{40,56},{48,64},{56,72},{64,... | collective-permute-start | bytes 1572872 | tf_op jit(solution)/shard_map/ppermute | solution.py:107
  112.7 41.4 %collective-permute-start.11 = (bf16[64,4096]{1,0:T(8,128)(2,1)S(1)}, bf16[64,4096]{1,0:T(8,128)(2,1)S(1)}, u32[]{:S(2)}, u32[]{:S(2)}) collective-permute-start(bf16[64,4096]{1,0:T(8,128)(2,1)S(1)} %bitcast.31), channel_id=1, source_target_pairs={{0,240},{8,248},{16,0},{24,8},{32,16},{40,24},{48,32},{56,40},{64,... | collective-permute-start | bytes 1572872 | tf_op jit(solution)/shard_map/ppermute | solution.py:107
  120.0 64.6 %all-to-all-start.5 = ((f32[32,4,512]{2,1,0:T(4,128)}), f32[32,4,512]{2,1,0:T(4,128)S(1)}, u32[]{:S(2)}, u32[]{:S(2)}) async-start(f32[32,4,512]{2,1,0:T(4,128)} %reshape.33), calls=%async_computation.5 | async-start | bytes 524288 | tf_op jit(solution)/shard_map/all_to_all | solution.py:188
  148.2 13.9 %collective-permute-start.10 = (bf16[64,4096]{1,0:T(8,128)(2,1)S(1)}, bf16[64,4096]{1,0:T(8,128)(2,1)S(1)}, u32[]{:S(2)}, u32[]{:S(2)}) collective-permute-start(bf16[64,4096]{1,0:T(8,128)(2,1)S(1)} %bitcast.32), channel_id=1, source_target_pairs={{0,248},{8,0},{16,8},{24,16},{32,24},{40,32},{48,40},{56,48},{64,5... | collective-permute-start | bytes 1572872 | tf_op jit(solution)/shard_map/ppermute | solution.py:107
  148.5 16.1 %collective-permute-start.9 = (bf16[64,4096]{1,0:T(8,128)(2,1)S(1)}, bf16[64,4096]{1,0:T(8,128)(2,1)S(1)}, u32[]{:S(2)}, u32[]{:S(2)}) collective-permute-start(bf16[64,4096]{1,0:T(8,128)(2,1)S(1)} %bitcast.33), channel_id=1, source_target_pairs={{0,8},{8,16},{16,24},{24,32},{32,40},{40,48},{48,56},{56,64},{64,7... | collective-permute-start | bytes 1572872 | tf_op jit(solution)/shard_map/ppermute | solution.py:107
  150.0 27.0 %collective-permute-start.8 = (bf16[64,4096]{1,0:T(8,128)(2,1)S(1)}, bf16[64,4096]{1,0:T(8,128)(2,1)S(1)}, u32[]{:S(2)}, u32[]{:S(2)}) collective-permute-start(bf16[64,4096]{1,0:T(8,128)(2,1)S(1)} %bitcast.34), channel_id=1, source_target_pairs={{0,16},{8,24},{16,32},{24,40},{32,48},{40,56},{48,64},{56,72},{64,... | collective-permute-start | bytes 1572872 | tf_op jit(solution)/shard_map/ppermute | solution.py:107
  (2 other events, 1.3 us)

commit v2 on v0

v2 whole, which is shorter than its diff:
```python
import functools

import jax
import jax.numpy as jnp
from jax import lax
from jax.experimental import pallas as pl
from jax.experimental.pallas import tpu as pltpu
from jax.sharding import PartitionSpec as P

GROUP = 8
CHUNKS = 2
MESH = pl.DeviceIdType.MESH
VMEM = pl.BlockSpec(memory_space=pltpu.VMEM)
SMEM = pl.BlockSpec(memory_space=pltpu.SMEM)
ANY = pl.BlockSpec(memory_space=pl.ANY)
TAIL = (((1,), (1,)), ((), ()))
BF16, F32 = jnp.bfloat16, jnp.float32


class Copies:
    def __init__(self, sent, landed):
        self.sent, self.landed, self.used = sent, landed, 0
        self.all = []

    def make(self, src, dst, node, feat):
        k = self.used
        self.used += 1
        copy = pltpu.make_async_remote_copy(
            src_ref=src,
            dst_ref=dst,
            send_sem=self.sent.at[k],
            recv_sem=self.landed.at[k],
            device_id=(node, feat),
            device_id_type=MESH,
        )
        self.all.append(copy)
        copy.start()
        return copy


def kernel(shape, *refs):
    slots, block, offsets, nodes, feats = shape
    (
        table, features, cotangent, tiles, weight_one, weight_two,
        layer_out, feature_grad, one_out, two_out,
        tile, chain_f, chain_b, feat_flat, cot_flat, feat_v, cot_v, one, two,
        sib_1, za_1, zd_1, relay_1, sib_2, za_2, zd_2, relay_2,
        out_1, out_2, comb_1, comb_2, got_1, got_2, own_1, own_2,
        agg_send, spread_send, agg, spread, up_send, back_send, up, back,
        pre_v, act_v, grads, got_grads, half, swapped, pieces, final, final_sib,
        local, sent, landed,
    ) = refs
    height, width = feat_flat.shape
    total_slots = offsets * slots
    blocks = width // block
    depth = agg.shape[0]
    share = agg.shape[1]
    ROWS, COLS, PREV_F, PREV_B = (k * total_slots for k in range(4))
    LAST_F = 4 * total_slots
    LAST_B = LAST_F + offsets * blocks
    none = total_slots

    me, mine = lax.axis_index("node"), lax.axis_index("feat")
    core = lax.rem(me, 2)
    sib = me + 1 - 2 * core
    ahead = lax.rem(me + 2 - 4 * core + nodes, nodes)
    behind = lax.rem(me - 2 + 4 * core + nodes, nodes)
    remote = Copies(sent, landed)

    loads = []
    for src, dst in (
        [(features, feat_flat), (cotangent, cot_flat)]
        + [
            (tiles.at[pl.ds(o * slots, slots)], tile.at[pl.ds(o * slots, slots)])
            for o in range(offsets)
        ]
        + [(weight_one, one), (weight_two, two)]
    ):
        copy = pltpu.make_async_copy(src, dst, local.at[len(loads)])
        copy.start()
        loads.append(copy)

    barrier = pltpu.get_barrier_semaphore()
    half_nodes = nodes // 2

    def greet(node, feat):
        pl.semaphore_signal(barrier, inc=1, device_id=(node, feat), device_id_type=MESH)

    greet(sib, mine)
    for d in range(1, half_nodes):
        greet(lax.rem(me + 2 * d, nodes), mine)
    for d in range(1, feats):
        greet(me, lax.rem(mine + d, feats))
    pl.semaphore_wait(barrier, half_nodes + feats - 1)

    def send_panel(panel, za, zd, sb):
        rows = blocks // CHUNKS
        parts = [
            remote.make(
                panel.at[pl.ds(k * rows, rows)], zd.at[pl.ds(k * rows, rows)], behind, mine
            )
            for k in range(CHUNKS)
        ]
        a = remote.make(panel, za, ahead, mine)
        s = remote.make(panel, sb, sib, mine)
        return parts, a, s

    def pass_on(parts, zd, relay):
        rows = blocks // CHUNKS
        relays = []
        for k, part in enumerate(parts):
            part.wait_recv()
            relays.append(
                remote.make(
                    zd.at[pl.ds(k * rows, rows)], relay.at[pl.ds(k * rows, rows)], sib, mine
                )
            )
        return relays

    def products(panel, o, take, prev, chain, contract):
        def step(g, carry):
            parts = []
            for i in range(GROUP):
                t = o * slots + g * GROUP + i
                parts.append(
                    lax.dot_general(
                        panel[table[take + t]],
                        tile[t],
                        contract,
                        preferred_element_type=F32,
                    )
                )
            for i in range(GROUP):
                t = o * slots + g * GROUP + i
                chain[t] = parts[i] + chain[table[prev + t]]
            return carry

        lax.fori_loop(0, slots // GROUP, step, 0)

    def forward(panel, o):
        products(panel, o, COLS, PREV_F, chain_f, TAIL)

    def gather_forward(out):
        def step(r, carry):
            total = chain_f[table[LAST_F + r]]
            for o in range(1, offsets):
                total = total + chain_f[table[LAST_F + o * blocks + r]]
            out[:, pl.ds(pl.multiple_of(r * block, block), block)] = total.astype(out.dtype)
            return carry

        lax.fori_loop(0, blocks, step, 0)

    def backward(panel, o, out):
        products(panel, o, ROWS, PREV_B, chain_b, (((1,), (0,)), ((), ())))

        def step(r, carry):
            part = chain_b[table[LAST_B + o * blocks + r]]
            out[:, pl.ds(pl.multiple_of(r * block, block), block)] = part.astype(out.dtype)
            return carry

        lax.fori_loop(0, blocks, step, 0)

    def spread_out(panel, out, comb, got, own):
        p_dir, p_comb, p_add, p_sib = (out.at[k] for k in range(4))
        backward(panel, 4 * core, p_dir)
        c_dir = remote.make(p_dir, got.at[0], behind, mine)
        backward(panel, 1 + 2 * core, p_comb)
        c_comb = remote.make(p_comb, comb, sib, mine)
        backward(panel, 4 - 4 * core, p_add)
        c_comb.wait_recv()
        p_add[...] = (p_add[...].astype(F32) + comb[...].astype(F32)).astype(BF16)
        c_add = remote.make(p_add, got.at[1], ahead, mine)
        backward(panel, 3 - 2 * core, p_sib)
        c_sib = remote.make(p_sib, got.at[2], sib, mine)
        backward(panel, 2, own)
        return c_dir, c_add, c_sib

    def collect(copies, got, own, out):
        for copy in copies:
            copy.wait_recv()
        total = own[...]
        for k in range(3):
            total = total + got[k].astype(F32)
        out[...] = total.astype(out.dtype)

    def rows_of(k):
        return pl.ds(pl.multiple_of(k * height, height), height)

    def columns_of(k):
        return pl.ds(pl.multiple_of(k * share, share), share)

    def to_rows(src, dst):
        copies = []
        for d in range(1, feats):
            peer = lax.rem(mine + d, feats)
            copies.append(
                remote.make(src.at[:, columns_of(peer)], dst.at[rows_of(mine)], me, peer)
            )
        dst[rows_of(mine)] = src[:, columns_of(mine)]
        return copies

    def to_features(src, dst):
        kept = share // block
        place = pl.ds(mine * kept, kept)
        copies = []
        for d in range(1, feats):
            peer = lax.rem(mine + d, feats)
            copies.append(remote.make(src.at[:, rows_of(peer)], dst.at[place], me, peer))
        dst[place] = src[:, rows_of(mine)]
        return copies

    def by_blocks(flat, panel):
        def step(r, carry):
            panel[r] = flat[:, pl.ds(pl.multiple_of(r * block, block), block)]
            return carry

        lax.fori_loop(0, blocks, step, 0)

    def put_blocks(value, out):
        for k in range(share // block):
            out[k] = value[:, k * block : (k + 1) * block]

    def arrived(copies):
        for copy in copies:
            copy.wait_recv()

    loads[0].wait()
    by_blocks(feat_flat, feat_v)
    parts, c_za, c_sb = send_panel(feat_v, za_1, zd_1, sib_1)
    chain_f[none] = jnp.zeros(chain_f.shape[1:], F32)
    chain_b[none] = jnp.zeros(chain_b.shape[1:], F32)
    loads[1].wait()
    by_blocks(cot_flat, cot_v)
    for copy in loads[2 : offsets + 2]:
        copy.wait()
    sums = spread_out(cot_v, out_1, comb_1, got_1, own_1)
    forward(feat_v, 2)
    c_sb.wait_recv()
    forward(sib_1, 3 - 2 * core)
    relays = pass_on(parts, zd_1, relay_1)
    forward(zd_1, 4 - 4 * core)
    c_za.wait_recv()
    forward(za_1, 4 * core)
    arrived(relays)
    forward(relay_1, 1 + 2 * core)
    gather_forward(agg_send)
    agg_copies = to_rows(agg_send, agg)
    collect(sums, got_1, own_1, spread_send)
    spread_copies = to_rows(spread_send, spread)

    dot = functools.partial(jnp.dot, preferred_element_type=F32)
    lead = (((0,), (0,)), ((), ()))
    loads[offsets + 2].wait()
    loads[offsets + 3].wait()
    arrived(agg_copies)
    pre = lax.dot_general(one[...], agg[...], lead, preferred_element_type=F32)
    pre_v[...] = pre
    act_v[...] = (pre * (1.0 / (1.0 + jnp.exp(-pre)))).astype(BF16)
    put_blocks(
        lax.dot_general(two[...], act_v[...], lead, preferred_element_type=F32).astype(BF16),
        up_send,
    )
    up_copies = to_features(up_send, up)
    arrived(spread_copies)
    act_back = dot(two[...], spread[...]).astype(BF16).astype(F32)
    pre = pre_v[...]
    sigma = 1.0 / (1.0 + jnp.exp(-pre))
    pre_back = (act_back * sigma * (1.0 + pre * (1.0 - sigma))).astype(BF16)
    put_blocks(dot(one[...], pre_back).astype(BF16), back_send)
    back_copies = to_features(back_send, back)
    grads[0] = lax.dot_general(agg[...], pre_back, TAIL, preferred_element_type=F32).astype(BF16)
    arrived(up_copies)
    parts, c_za, c_sb = send_panel(up, za_2, zd_2, sib_2)
    grads[1] = lax.dot_general(
        act_v[...], spread[...], TAIL, preferred_element_type=F32
    ).astype(BF16)

    arrived(back_copies)
    sums = spread_out(back, out_2, comb_2, got_2, own_2)
    grad_copies = []
    for d in range(1, feats):
        peer = lax.rem(mine + d, feats)
        grad_copies.append(
            remote.make(grads.at[:, rows_of(peer)], got_grads.at[d - 1], me, peer)
        )
    forward(up, 2)
    c_sb.wait_recv()
    forward(sib_2, 3 - 2 * core)
    relays = pass_on(parts, zd_2, relay_2)
    arrived(grad_copies)
    total = grads[:, rows_of(mine)].astype(F32)
    for d in range(feats - 1):
        total = total + got_grads[d].astype(F32)
    half[...] = total
    swap = remote.make(half.at[1 - core], swapped, sib, mine)
    forward(zd_2, 4 - 4 * core)
    swap.wait_recv()
    swapped[...] = swapped[...] + half[core]
    groups = min(half_nodes, height // 8)
    splits = half_nodes // groups
    tall, wide = height // groups, depth // splits

    def piece(k):
        row, column = k // splits, lax.rem(k, splits)
        return (
            pl.ds(pl.multiple_of(row * tall, tall), tall),
            pl.ds(pl.multiple_of(column * wide, wide), wide),
        )

    place = me // 2
    piece_copies = []
    for d in range(1, half_nodes):
        peer = lax.rem(place + d, half_nodes)
        piece_copies.append(
            remote.make(
                swapped.at[piece(peer)], pieces.at[d - 1], 2 * peer + core, mine
            )
        )
    c_za.wait_recv()
    forward(za_2, 4 * core)
    arrived(piece_copies)
    total = swapped[piece(place)]
    for d in range(half_nodes - 1):
        total = total + pieces[d]
    final[piece(place)] = total
    final_copies = []
    for d in range(1, half_nodes):
        peer = lax.rem(place + d, half_nodes)
        final_copies.append(
            remote.make(
                final.at[piece(place)], final.at[piece(place)], 2 * peer + core, mine
            )
        )
    arrived(relays)
    forward(relay_2, 1 + 2 * core)
    gather_forward(layer_out)
    arrived(final_copies)
    last = remote.make(final, final_sib, sib, mine)
    collect(sums, got_2, own_2, feature_grad)
    last.wait_recv()

    @pl.when(core == 0)
    def _():
        one_out[...] = final[...]
        two_out[...] = final_sib[...]

    @pl.when(core == 1)
    def _():
        one_out[...] = final_sib[...]
        two_out[...] = final[...]

    for copy in remote.all:
        copy.wait_send()


def links(keys, live, blocks):
    offsets, slots = keys.shape
    place = jnp.arange(slots, dtype=jnp.int32)
    base = (jnp.arange(offsets, dtype=jnp.int32) * slots)[:, None]
    none = offsets * slots
    same = (keys[:, :, None] == keys[:, None, :]) & (place[None, :, None] > place[None, None, :])
    prev = jnp.max(jnp.where(same, place[None, None, :], -1), axis=2)
    owns = (keys[:, None, :] == jnp.arange(blocks, dtype=jnp.int32)[None, :, None]) & live[
        :, None, :
    ]
    last = jnp.max(jnp.where(owns, place[None, None, :], -1), axis=2)
    return jnp.where(prev < 0, none, prev + base), jnp.where(last < 0, none, last + base)


def on_device(features, tiles, tile_rows, tile_cols, counts, weight_one, weight_two, cotangent):
    offsets = counts.shape[0]
    slots = tile_rows.shape[0] // offsets
    block = tiles.shape[-1]
    height, width = features.shape
    depth = weight_one.shape[0]
    nodes, feats = lax.axis_size("node"), lax.axis_size("feat")
    share = width // feats
    rows, cols = tile_rows.reshape(offsets, slots), tile_cols.reshape(offsets, slots)
    live = jnp.arange(slots, dtype=jnp.int32)[None, :] < counts[:, None]
    prev_f, last_f = links(rows, live, width // block)
    prev_b, last_b = links(cols, live, width // block)
    table = jnp.concatenate(
        [t.reshape(-1) for t in (rows, cols, prev_f, prev_b, last_f, last_b)]
    )
    half_nodes = nodes // 2
    groups = min(half_nodes, height // 8)
    piece = (height // groups, depth * groups // half_nodes)
    remote_copies = 2 * (4 + 2 * CHUNKS - 2 + 4) + 5 * (feats - 1) + 2 + 2 * (half_nodes - 1)
    flat = pltpu.VMEM((height, width), BF16)
    panel = pltpu.VMEM((width // block, height, block), BF16)
    stack = pltpu.VMEM((share // block, depth, block), BF16)
    chain = pltpu.VMEM((offsets * slots + 1, height, block), F32)
    square = pltpu.VMEM((depth, depth), BF16)
    side = pltpu.VMEM((depth, share), BF16)
    return pl.pallas_call(
        functools.partial(kernel, (slots, block, offsets, nodes, feats)),
        out_shape=[jax.ShapeDtypeStruct((height, width), BF16)] * 2
        + [jax.ShapeDtypeStruct((height, depth), F32)] * 2,
        in_specs=[SMEM] + [ANY] * 5,
        out_specs=[VMEM] * 4,
        scratch_shapes=[pltpu.VMEM(tiles.shape, BF16), chain, chain]
        + [flat, flat, panel, panel, square, square]
        + [panel] * 8
        + [pltpu.VMEM((4, height, width), BF16)] * 2
        + [flat] * 2
        + [pltpu.VMEM((3, height, width), BF16)] * 2
        + [pltpu.VMEM((height, width), F32)] * 2
        + [flat, flat, side, side, stack, stack, panel, panel]
        + [
            pltpu.VMEM((depth, share), F32),
            side,
            pltpu.VMEM((2, depth, depth), BF16),
            pltpu.VMEM((feats - 1, 2, height, depth), BF16),
            pltpu.VMEM((2, height, depth), F32),
            pltpu.VMEM((height, depth), F32),
            pltpu.VMEM((half_nodes - 1, *piece), F32),
            pltpu.VMEM((height, depth), F32),
            pltpu.VMEM((height, depth), F32),
            pltpu.SemaphoreType.DMA((offsets + 4,)),
            pltpu.SemaphoreType.DMA((remote_copies,)),
            pltpu.SemaphoreType.DMA((remote_copies,)),
        ],
        compiler_params=pltpu.CompilerParams(
            collective_id=0, has_side_effects=True, vmem_limit_bytes=60 << 20
        ),
    )(table, features, cotangent, tiles, weight_one, weight_two)


def solution(mesh):
    in_specs = (
        P("feat", "node"),
        P("node", None, None),
        P("node"),
        P("node"),
        P("node"),
        P(),
        P(),
        P("feat", "node"),
    )
    out_specs = (P("feat", "node"), P("feat", "node"), P("feat", None), P("feat", None))
    return jax.shard_map(
        on_device, mesh=mesh, in_specs=in_specs, out_specs=out_specs, check_vma=False
    )
```

time: 616 us -> 140 us (0.23); the launches traced: 608 us -> 140 us
  waiting for transfers between devices: 333 us -> 0 us
  Pallas kernels: 0 us -> 128 us
  matrix products: 104 us -> 0 us
  starting transfers between devices: 81.1 us -> 0 us
  local copies, waits for them, and re-layouts: 66.5 us -> 10.1 us
  between operations: 14.7 us -> 0.67 us
  other arithmetic: 9.75 us -> 1.49 us
    psum x1 -> x0, waiting for transfers between devices: 262 us -> none  [on_device(): one_grad, two_grad = lax.psum((one_rows, two_rows), 'node')]
    pallas_call x0 -> x1, Pallas kernels: none -> 128 us  [on_device(): pl.pallas_call(functools.partial(kernel, (slots, block, offsets, nodes, f...]
    dot_general x46 -> x0, matrix products: 104 us -> none  [the longest x10 33.8 us: forward_term(): jnp.einsum('hsk,srk->hsr', pieces, tile_set, preferred_element_type=jnp.f...]
    reduce_scatter x2 -> x0, waiting for transfers between devices: 44.9 us -> none  [the longest x1 44.9 us: on_device(): lax.psum_scatter(two_part, 'feat', scatter_dimension=0, tiled=True)]
    ppermute x16 -> x0, starting transfers between devices: 40.8 us -> none  [passed_along(): return lax.ppermute(value, axis, pairs)]
    all_to_all x8 -> x0, starting transfers between devices: 40.3 us -> none  [the longest x4 21 us: to_features(): lax.all_to_all(field, 'feat', split_axis=0, concat_axis=1, tiled=True)]
    gather x20 -> x0, local copies, waits for them, and re-layouts: 28.1 us -> none  [the longest x10 14.1 us: backward_term(): jnp.take(panel.reshape(width, blocks_count, block), slot_rows, axis=1)]
    all_to_all x8 -> x0, waiting for transfers between devices: 19.2 us -> none  [the longest x4 15.2 us: to_rows(): lax.all_to_all(field, 'feat', split_axis=1, concat_axis=0, tiled=True)]
  transfers between devices with their start and end apart: 27 -> 0, of which waited for: 6 -> 0; matrix products, arithmetic and copies ran while one was open for 27% -> 0% of each run, Pallas kernels for 0% -> 0%
where the time goes in v2:
time: 140 us
  Pallas kernels  128 us (91%)
  local copies, waits for them, and re-layouts  10.1 us (7%)
  other arithmetic  1.49 us (1%)
    pallas_call x1, Pallas kernels, on_device(): pl.pallas_call(functools.partial(kernel, (slots, block, offsets, nodes, f...  128 us
    unnamed x4, local copies, waits for them, and re-layouts  6.87 us

profile of v2, /device:TPU:25, one launch (start us, length us, event | category | flops | bytes accessed | tf_op | source)
XLA Modules:
  0.0 140.0 jit_solution(15770034597503385603)
XLA Ops:
  0.6 0.7 iota_compare_fusion.3
  1.4 0.8 eq.56
  2.1 0.8 eq.60
  2.9 0.4 select_reduce_fusion
  3.3 0.2 select_reduce_fusion.2
  3.5 0.1 add_select_fusion.2
  3.6 0.1 add_select_fusion
  3.6 0.1 select_n.55
  3.7 0.1 select_n.49
  3.8 0.1 select_n.46
  3.9 0.1 select_n.52
  4.0 1.4 concatenate.3.refs_0_
  5.3 127.8 %shard_map.111 = (bf16[64,4096]{1,0:T(8,128)(2,1)}, bf16[64,4096]{1,0:T(8,128)(2,1)}, f32[64,512]{1,0:T(8,128)}, f32[64,512]{1,0:T(8,128)}) custom-call(s32[1280]{0:T(1024)} %concatenate.3.refs_0_, bf16[64,4096]{1,0:T(8,128)(2,1)} %refs_1_.1, bf16[64,4096]{1,0:T(8,128)(2,1)} %refs_2_.1, bf16[240,128,128]{2,1,0:T(8,128)(2,1)} %refs_3_.1, ...), custom_call_target="tpu_custom_call" | custom-call | tf_op jit(solution)/shard_map/pallas_call | solution.py:395
  133.1 1.9 %copy.16 = bf16[64,4096]{1,0:T(8,128)(2,1)} copy(bf16[64,4096]{1,0:T(8,128)(2,1)} %get-tuple-element.16) | data formatting | bytes 1048576
  135.0 1.9 %copy.17 = bf16[64,4096]{1,0:T(8,128)(2,1)} copy(bf16[64,4096]{1,0:T(8,128)(2,1)} %get-tuple-element.17) | data formatting | bytes 1048576
  136.9 1.6 %copy.18 = f32[64,512]{1,0:T(8,128)} copy(f32[64,512]{1,0:T(8,128)} %get-tuple-element.18) | data formatting | bytes 262144
  138.5 1.6 %copy.19 = f32[64,512]{1,0:T(8,128)} copy(f32[64,512]{1,0:T(8,128)} %get-tuple-element.19) | data formatting | bytes 262144
  (2 shorter events, 0.0 us)

commit v3 on v2

--- a/solution.py
+++ b/solution.py
@@ -9,6 +9,7 @@
 
 GROUP = 8
 CHUNKS = 2
+SIDES = 2
 MESH = pl.DeviceIdType.MESH
 VMEM = pl.BlockSpec(memory_space=pltpu.VMEM)
 SMEM = pl.BlockSpec(memory_space=pltpu.SMEM)
@@ -17,37 +18,84 @@
 BF16, F32 = jnp.bfloat16, jnp.float32
 
 
+class Copy:
+    def __init__(self, copy):
+        self.copy, self.left = copy, False
+        copy.start()
+
+    def wait_recv(self):
+        self.copy.wait_recv()
+
+    def wait_send(self):
+        if not self.left:
+            self.copy.wait_send()
+        self.left = True
+
+
 class Copies:
     def __init__(self, sent, landed):
-        self.sent, self.landed, self.used = sent, landed, 0
-        self.all = []
+        self.sent, self.landed, self.all = sent, landed, []
 
     def make(self, src, dst, node, feat):
-        k = self.used
-        self.used += 1
-        copy = pltpu.make_async_remote_copy(
-            src_ref=src,
-            dst_ref=dst,
-            send_sem=self.sent.at[k],
-            recv_sem=self.landed.at[k],
-            device_id=(node, feat),
-            device_id_type=MESH,
+        k = len(self.all)
+        copy = Copy(
+            pltpu.make_async_remote_copy(
+                src_ref=src,
+                dst_ref=dst,
+                send_sem=self.sent.at[k],
+                recv_sem=self.landed.at[k],
+                device_id=(node, feat),
+                device_id_type=MESH,
+            )
         )
         self.all.append(copy)
-        copy.start()
         return copy
+
+
+def table_kernel(slots, blocks, counts, rows_v, cols_v, table_v):
+    offsets, total = counts.shape[0], rows_v.shape[1]
+    iota = functools.partial(lax.broadcasted_iota, jnp.int32)
+    down, along = iota((total, total), 0), iota((total, total), 1)
+
+    def place(index, size, count):
+        group = jnp.zeros_like(index)
+        for k in range(1, count):
+            group = group + (index >= k * size).astype(jnp.int32)
+        return group
+
+    close = (down < along) & (place(down, slots, offsets) == place(along, slots, offsets))
+    line = iota((total, 1), 0)
+    owner = place(line, slots, offsets)
+    limit = jnp.zeros_like(line)
+    for o in range(offsets):
+        limit = jnp.where(owner == o, o * slots + counts[o], limit)
+    spots = iota((1, offsets * blocks), 1)
+    group = place(spots, blocks, offsets)
+    for keys_v, prev, last in ((rows_v, 0, 2), (cols_v, 1, 3)):
+        keys = keys_v[...].astype(F32)
+        column = jnp.sum(jnp.where(down == along, keys, 0.0), axis=1, keepdims=True)
+        where = jnp.max(
+            jnp.where(close & (column == keys), down.astype(F32), -1.0), axis=0, keepdims=True
+        ).astype(jnp.int32)
+        table_v[prev : prev + 1, :total] = jnp.where(where < 0, total, where)
+        wanted = (spots - group * blocks).astype(F32)
+        mine = (column == wanted) & (owner == group) & (line < limit)
+        where = jnp.max(
+            jnp.where(mine, line.astype(F32), -1.0), axis=0, keepdims=True
+        ).astype(jnp.int32)
+        table_v[last : last + 1, : offsets * blocks] = jnp.where(where < 0, total, where)
 
 
 def kernel(shape, *refs):
     slots, block, offsets, nodes, feats = shape
     (
-        table, features, cotangent, tiles, weight_one, weight_two,
+        rows, cols, table, features, cotangent, tiles, weight_one, weight_two,
         layer_out, feature_grad, one_out, two_out,
         tile, chain_f, chain_b, feat_flat, cot_flat, feat_v, cot_v, one, two,
         sib_1, za_1, zd_1, relay_1, sib_2, za_2, zd_2, relay_2,
         out_1, out_2, comb_1, comb_2, got_1, got_2, own_1, own_2,
         agg_send, spread_send, agg, spread, up_send, back_send, up, back,
-        pre_v, act_v, grads, got_grads, half, swapped, pieces, final, final_sib,
+        pre_v, act_v, grads, grad_sib, grad_chip, got_y, half, swapped, pieces, final, final_sib,
         local, sent, landed,
     ) = refs
     height, width = feat_flat.shape
@@ -55,9 +103,7 @@
     blocks = width // block
     depth = agg.shape[0]
     share = agg.shape[1]
-    ROWS, COLS, PREV_F, PREV_B = (k * total_slots for k in range(4))
-    LAST_F = 4 * total_slots
-    LAST_B = LAST_F + offsets * blocks
+    PREV_F, PREV_B, LAST_F, LAST_B = range(4)
     none = total_slots
 
     me, mine = lax.axis_index("node"), lax.axis_index("feat")
@@ -80,6 +126,13 @@
         copy.start()
         loads.append(copy)
 
+    def by_blocks(flat, panel):
+        def step(r, carry):
+            panel[r] = flat[:, pl.ds(pl.multiple_of(r * block, block), block)]
+            return carry
+
+        lax.fori_loop(0, blocks, step, 0)
+
     barrier = pltpu.get_barrier_semaphore()
     half_nodes = nodes // 2
 
@@ -91,6 +144,8 @@
         greet(lax.rem(me + 2 * d, nodes), mine)
     for d in range(1, feats):
         greet(me, lax.rem(mine + d, feats))
+    loads[0].wait()
+    by_blocks(feat_flat, feat_v)
     pl.semaphore_wait(barrier, half_nodes + feats - 1)
 
     def send_panel(panel, za, zd, sb):
@@ -124,7 +179,7 @@
                 t = o * slots + g * GROUP + i
                 parts.append(
                     lax.dot_general(
-                        panel[table[take + t]],
+                        panel[take[t]],
                         tile[t],
                         contract,
                         preferred_element_type=F32,
@@ -132,48 +187,53 @@
                 )
             for i in range(GROUP):
                 t = o * slots + g * GROUP + i
-                chain[t] = parts[i] + chain[table[prev + t]]
+                chain[t] = parts[i] + chain[table[prev, t]]
             return carry
 
         lax.fori_loop(0, slots // GROUP, step, 0)
 
     def forward(panel, o):
-        products(panel, o, COLS, PREV_F, chain_f, TAIL)
+        products(panel, o, cols, PREV_F, chain_f, TAIL)
 
     def gather_forward(out):
         def step(r, carry):
-            total = chain_f[table[LAST_F + r]]
+            total = chain_f[table[LAST_F, r]]
             for o in range(1, offsets):
-                total = total + chain_f[table[LAST_F + o * blocks + r]]
+                total = total + chain_f[table[LAST_F, o * blocks + r]]
             out[:, pl.ds(pl.multiple_of(r * block, block), block)] = total.astype(out.dtype)
             return carry
 
         lax.fori_loop(0, blocks, step, 0)
 
     def backward(panel, o, out):
-        products(panel, o, ROWS, PREV_B, chain_b, (((1,), (0,)), ((), ())))
+        products(panel, o, rows, PREV_B, chain_b, (((1,), (0,)), ((), ())))
 
         def step(r, carry):
-            part = chain_b[table[LAST_B + o * blocks + r]]
+            part = chain_b[table[LAST_B, o * blocks + r]]
             out[:, pl.ds(pl.multiple_of(r * block, block), block)] = part.astype(out.dtype)
             return carry
 
         lax.fori_loop(0, blocks, step, 0)
 
-    def spread_out(panel, out, comb, got, own):
+    def spread_early(panel, out, comb, got):
         p_dir, p_comb, p_add, p_sib = (out.at[k] for k in range(4))
-        backward(panel, 4 * core, p_dir)
-        c_dir = remote.make(p_dir, got.at[0], behind, mine)
         backward(panel, 1 + 2 * core, p_comb)
         c_comb = remote.make(p_comb, comb, sib, mine)
+        backward(panel, 4 * core, p_dir)
         backward(panel, 4 - 4 * core, p_add)
+        backward(panel, 3 - 2 * core, p_sib)
+        return c_comb, remote.make(p_sib, got.at[2], sib, mine)
+
+    def spread_late(before, c_comb, out, comb, got):
+        parts, a = before
+        p_dir, p_add = out.at[0], out.at[2]
+        for part in parts:
+            part.wait_send()
+        c_dir = remote.make(p_dir, got.at[0], behind, mine)
         c_comb.wait_recv()
         p_add[...] = (p_add[...].astype(F32) + comb[...].astype(F32)).astype(BF16)
-        c_add = remote.make(p_add, got.at[1], ahead, mine)
-        backward(panel, 3 - 2 * core, p_sib)
-        c_sib = remote.make(p_sib, got.at[2], sib, mine)
-        backward(panel, 2, own)
-        return c_dir, c_add, c_sib
+        a.wait_send()
+        return c_dir, remote.make(p_add, got.at[1], ahead, mine)
 
     def collect(copies, got, own, out):
         for copy in copies:
@@ -209,13 +269,6 @@
         dst[place] = src[:, rows_of(mine)]
         return copies
 
-    def by_blocks(flat, panel):
-        def step(r, carry):
-            panel[r] = flat[:, pl.ds(pl.multiple_of(r * block, block), block)]
-            return carry
-
-        lax.fori_loop(0, blocks, step, 0)
-
     def put_blocks(value, out):
         for k in range(share // block):
             out[k] = value[:, k * block : (k + 1) * block]
@@ -224,8 +277,6 @@
         for copy in copies:
             copy.wait_recv()
 
-    loads[0].wait()
-    by_blocks(feat_flat, feat_v)
     parts, c_za, c_sb = send_panel(feat_v, za_1, zd_1, sib_1)
     chain_f[none] = jnp.zeros(chain_f.shape[1:], F32)
     chain_b[none] = jnp.zeros(chain_b.shape[1:], F32)
@@ -233,10 +284,11 @@
     by_blocks(cot_flat, cot_v)
     for copy in loads[2 : offsets + 2]:
         copy.wait()
-    sums = spread_out(cot_v, out_1, comb_1, got_1, own_1)
+    c_comb, c_own = spread_early(cot_v, out_1, comb_1, got_1)
     forward(feat_v, 2)
     c_sb.wait_recv()
     forward(sib_1, 3 - 2 * core)
+    sums = (c_own, *spread_late((parts, c_za), c_comb, out_1, comb_1, got_1))
     relays = pass_on(parts, zd_1, relay_1)
     forward(zd_1, 4 - 4 * core)
     c_za.wait_recv()
@@ -245,6 +297,7 @@
     forward(relay_1, 1 + 2 * core)
     gather_forward(agg_send)
     agg_copies = to_rows(agg_send, agg)
+    backward(cot_v, 2, own_1)
     collect(sums, got_1, own_1, spread_send)
     spread_copies = to_rows(spread_send, spread)
 
@@ -267,35 +320,50 @@
     sigma = 1.0 / (1.0 + jnp.exp(-pre))
     pre_back = (act_back * sigma * (1.0 + pre * (1.0 - sigma))).astype(BF16)
     put_blocks(dot(one[...], pre_back).astype(BF16), back_send)
+    arrived(up_copies)
+    parts, c_za, c_sb = send_panel(up, za_2, zd_2, sib_2)
     back_copies = to_features(back_send, back)
     grads[0] = lax.dot_general(agg[...], pre_back, TAIL, preferred_element_type=F32).astype(BF16)
-    arrived(up_copies)
-    parts, c_za, c_sb = send_panel(up, za_2, zd_2, sib_2)
     grads[1] = lax.dot_general(
         act_v[...], spread[...], TAIL, preferred_element_type=F32
     ).astype(BF16)
-
+    c_grad = remote.make(grads.at[1 - core], grad_sib, sib, mine)
+
+    forward(up, 2)
+    c_grad.wait_recv()
+    side = feats // SIDES * height
+    added = grads[core].astype(F32) + grad_sib[...].astype(F32)
+    for k in range(SIDES):
+        grad_chip[k] = added[k * side : (k + 1) * side].astype(BF16)
+    ring = feats // SIDES
+    near, far = lax.rem(mine, ring), mine // ring
     arrived(back_copies)
-    sums = spread_out(back, out_2, comb_2, got_2, own_2)
-    grad_copies = []
-    for d in range(1, feats):
-        peer = lax.rem(mine + d, feats)
-        grad_copies.append(
-            remote.make(grads.at[:, rows_of(peer)], got_grads.at[d - 1], me, peer)
+    ring_copies = []
+    for d in range(1, ring):
+        peer = lax.rem(near + d, ring)
+        ring_copies.append(
+            remote.make(grad_chip.at[:, rows_of(peer)], got_y.at[d - 1], me, far * ring + peer)
         )
-    forward(up, 2)
-    c_sb.wait_recv()
-    forward(sib_2, 3 - 2 * core)
+    p_dir, p_comb, p_add, p_sib = (out_2.at[k] for k in range(4))
+    backward(back, 4 * core, p_dir)
+    c_dir = remote.make(p_dir, got_2.at[0], behind, mine)
+    backward(back, 1 + 2 * core, p_comb)
+    c_comb = remote.make(p_comb, comb_2, sib, mine)
+    backward(back, 4 - 4 * core, p_add)
+    c_comb.wait_recv()
+    p_add[...] = (p_add[...].astype(F32) + comb_2[...].astype(F32)).astype(BF16)
+    c_add = remote.make(p_add, got_2.at[1], ahead, mine)
+    arrived(ring_copies)
+    total = grad_chip[:, rows_of(near)].astype(F32)
+    for d in range(ring - 1):
+        total = total + got_y[d].astype(F32)
+    half[...] = total
+    swap = remote.make(half.at[1 - far], swapped, me, (1 - far) * ring + near)
+    backward(back, 3 - 2 * core, p_sib)
+    sums = c_dir, c_add, remote.make(p_sib, got_2.at[2], sib, mine)
     relays = pass_on(parts, zd_2, relay_2)
-    arrived(grad_copies)
-    total = grads[:, rows_of(mine)].astype(F32)
-    for d in range(feats - 1):
-        total = total + got_grads[d].astype(F32)
-    half[...] = total
-    swap = remote.make(half.at[1 - core], swapped, sib, mine)
-    forward(zd_2, 4 - 4 * core)
     swap.wait_recv()
-    swapped[...] = swapped[...] + half[core]
+    swapped[...] = swapped[...] + half[far]
     groups = min(half_nodes, height // 8)
     splits = half_nodes // groups
     tall, wide = height // groups, depth // splits
@@ -316,8 +384,8 @@
                 swapped.at[piece(peer)], pieces.at[d - 1], 2 * peer + core, mine
             )
         )
-    c_za.wait_recv()
-    forward(za_2, 4 * core)
+    c_sb.wait_recv()
+    forward(sib_2, 3 - 2 * core)
     arrived(piece_copies)
     total = swapped[piece(place)]
     for d in range(half_nodes - 1):
@@ -331,13 +399,17 @@
                 final.at[piece(place)], final.at[piece(place)], 2 * peer + core, mine
             )
         )
+    c_za.wait_recv()
+    forward(za_2, 4 * core)
+    forward(zd_2, 4 - 4 * core)
+    arrived(final_copies)
+    last = remote.make(final, final_sib, sib, mine)
     arrived(relays)
     forward(relay_2, 1 + 2 * core)
     gather_forward(layer_out)
-    arrived(final_copies)
-    last = remote.make(final, final_sib, sib, mine)
+    backward(back, 2, own_2)
+    last.wait_recv()
     collect(sums, got_2, own_2, feature_grad)
-    last.wait_recv()
 
     @pl.when(core == 0)
     def _():
@@ -353,18 +425,16 @@
         copy.wait_send()
 
 
-def links(keys, live, blocks):
-    offsets, slots = keys.shape
-    place = jnp.arange(slots, dtype=jnp.int32)
-    base = (jnp.arange(offsets, dtype=jnp.int32) * slots)[:, None]
-    none = offsets * slots
-    same = (keys[:, :, None] == keys[:, None, :]) & (place[None, :, None] > place[None, None, :])
-    prev = jnp.max(jnp.where(same, place[None, None, :], -1), axis=2)
-    owns = (keys[:, None, :] == jnp.arange(blocks, dtype=jnp.int32)[None, :, None]) & live[
-        :, None, :
+def give_kernel(*refs):
+    half = (len(refs) - 1) // 2
+    copies = [
+        pltpu.make_async_copy(src, dst, refs[-1].at[k])
+        for k, (src, dst) in enumerate(zip(refs[:half], refs[half:-1]))
     ]
-    last = jnp.max(jnp.where(owns, place[None, None, :], -1), axis=2)
-    return jnp.where(prev < 0, none, prev + base), jnp.where(last < 0, none, last + base)
+    for copy in copies:
+        copy.start()
+    for copy in copies:
+        copy.wait()
 
 
 def on_device(features, tiles, tile_rows, tile_cols, counts, weight_one, weight_two, cotangent):
@@ -375,28 +445,30 @@
     depth = weight_one.shape[0]
     nodes, feats = lax.axis_size("node"), lax.axis_size("feat")
     share = width // feats
-    rows, cols = tile_rows.reshape(offsets, slots), tile_cols.reshape(offsets, slots)
-    live = jnp.arange(slots, dtype=jnp.int32)[None, :] < counts[:, None]
-    prev_f, last_f = links(rows, live, width // block)
-    prev_b, last_b = links(cols, live, width // block)
-    table = jnp.concatenate(
-        [t.reshape(-1) for t in (rows, cols, prev_f, prev_b, last_f, last_b)]
-    )
+    lanes = -(-max(tile_rows.shape[0], offsets * (width // block)) // 128) * 128
     half_nodes = nodes // 2
     groups = min(half_nodes, height // 8)
     piece = (height // groups, depth * groups // half_nodes)
-    remote_copies = 2 * (4 + 2 * CHUNKS - 2 + 4) + 5 * (feats - 1) + 2 + 2 * (half_nodes - 1)
+    remote_copies = (
+        2 * (2 * CHUNKS + 6) + 4 * (feats - 1) + feats // SIDES - 1 + 3 + 2 * (half_nodes - 1)
+    )
     flat = pltpu.VMEM((height, width), BF16)
     panel = pltpu.VMEM((width // block, height, block), BF16)
     stack = pltpu.VMEM((share // block, depth, block), BF16)
     chain = pltpu.VMEM((offsets * slots + 1, height, block), F32)
     square = pltpu.VMEM((depth, depth), BF16)
     side = pltpu.VMEM((depth, share), BF16)
-    return pl.pallas_call(
+    table = pl.pallas_call(
+        functools.partial(table_kernel, slots, width // block),
+        out_shape=jax.ShapeDtypeStruct((8, lanes), jnp.int32),
+        in_specs=[SMEM, VMEM, VMEM],
+        out_specs=VMEM,
+    )(counts, tile_rows.reshape(1, -1), tile_cols.reshape(1, -1))
+    made = pl.pallas_call(
         functools.partial(kernel, (slots, block, offsets, nodes, feats)),
         out_shape=[jax.ShapeDtypeStruct((height, width), BF16)] * 2
         + [jax.ShapeDtypeStruct((height, depth), F32)] * 2,
-        in_specs=[SMEM] + [ANY] * 5,
+        in_specs=[SMEM] * 3 + [ANY] * 5,
         out_specs=[VMEM] * 4,
         scratch_shapes=[pltpu.VMEM(tiles.shape, BF16), chain, chain]
         + [flat, flat, panel, panel, square, square]
@@ -410,8 +482,10 @@
             pltpu.VMEM((depth, share), F32),
             side,
             pltpu.VMEM((2, depth, depth), BF16),
-            pltpu.VMEM((feats - 1, 2, height, depth), BF16),
-            pltpu.VMEM((2, height, depth), F32),
+            square,
+            pltpu.VMEM((SIDES, depth // SIDES, depth), BF16),
+            pltpu.VMEM((max(feats // SIDES - 1, 1), SIDES, height, depth), BF16),
+            pltpu.VMEM((SIDES, height, depth), F32),
             pltpu.VMEM((height, depth), F32),
             pltpu.VMEM((half_nodes - 1, *piece), F32),
             pltpu.VMEM((height, depth), F32),
@@ -423,7 +497,23 @@
         compiler_params=pltpu.CompilerParams(
             collective_id=0, has_side_effects=True, vmem_limit_bytes=60 << 20
         ),
-    )(table, features, cotangent, tiles, weight_one, weight_two)
+    )(
+        tile_rows,
+        tile_cols,
+        table,
+        features,
+        cotangent,
+        tiles,
+        weight_one,
+        weight_two,
+    )
+    return pl.pallas_call(
+        give_kernel,
+        out_shape=[jax.ShapeDtypeStruct(m.shape, m.dtype) for m in made],
+        in_specs=[ANY] * 4,
+        out_specs=[ANY] * 4,
+        scratch_shapes=[pltpu.SemaphoreType.DMA((4,))],
+    )(*made)
 
 
 def solution(mesh):

time: 140 us -> 156 us (1.11); the launches traced: 140 us -> 154 us
  Pallas kernels: 128 us -> 154 us
  local copies, waits for them, and re-layouts: 10.1 us -> 0 us
    pallas_call x0 -> x2, Pallas kernels: none -> 42.4 us  [the longest x1 40.8 us: on_device(): pl.pallas_call(give_kernel, out_shape=[jax.ShapeDtypeStruct(m.shape, m.dt...]
    pallas_call x1, Pallas kernels: 128 us -> 111 us  [on_device(): pl.pallas_call(functools.partial(kernel, (slots, block, offsets, nodes, f...]
    unnamed x4 -> x0, local copies, waits for them, and re-layouts: 6.87 us -> none
where the time goes in v3:
time: 156 us; the launch traced here: 154 us
  Pallas kernels  154 us (99%)
    pallas_call x1, Pallas kernels, on_device(): pl.pallas_call(functools.partial(kernel, (slots, block, offsets, nodes, f...  111 us
    pallas_call x1, Pallas kernels, on_device(): pl.pallas_call(give_kernel, out_shape=[jax.ShapeDtypeStruct(m.shape, m.dt...  40.8 us

profile of v3, /device:TPU:25, one launch (start us, length us, event | category | flops | bytes accessed | tf_op | source)
XLA Modules:
  0.0 154.2 jit_solution(8402850910627206218)
XLA Ops:
  0.6 1.5 shard_map.111.refs_2_
  2.2 111.2 %shard_map.112 = (bf16[64,4096]{1,0:T(8,128)(2,1)}, bf16[64,4096]{1,0:T(8,128)(2,1)}, f32[64,512]{1,0:T(8,128)}, f32[64,512]{1,0:T(8,128)}) custom-call(s32[240]{0:T(256)} %refs_0_.1, s32[240]{0:T(256)} %refs_1_.1, s32[8,256]{1,0:T(8,128)} %shard_map.111.refs_2_, bf16[64,4096]{1,0:T(8,128)(2,1)} %refs_3_.1, bf16[64,4096]{1,0:T(8,128)(2,1)} %refs_4_.1, ...), custom_call_target="tpu_custom_call" | custom-call | tf_op jit(solution)/shard_map/pallas_call | solution.py:467
  113.3 40.8 %shard_map.113 = (bf16[64,4096]{1,0:T(8,128)(2,1)}, bf16[64,4096]{1,0:T(8,128)(2,1)}, f32[64,512]{1,0:T(8,128)}, f32[64,512]{1,0:T(8,128)}) custom-call(bf16[64,4096]{1,0:T(8,128)(2,1)} %get-tuple-element.8.refs_0_, bf16[64,4096]{1,0:T(8,128)(2,1)} %get-tuple-element.9.refs_1_, f32[64,512]{1,0:T(8,128)} %get-tuple-element.10.refs_2_, ...), custom_call_target="tpu_custom_call" | custom-call | tf_op jit(solution)/shard_map/pallas_call | solution.py:510

commit v4 on v3

--- a/solution.py
+++ b/solution.py
@@ -95,7 +95,7 @@
         sib_1, za_1, zd_1, relay_1, sib_2, za_2, zd_2, relay_2,
         out_1, out_2, comb_1, comb_2, got_1, got_2, own_1, own_2,
         agg_send, spread_send, agg, spread, up_send, back_send, up, back,
-        pre_v, act_v, grads, grad_sib, grad_chip, got_y, half, swapped, pieces, final, final_sib,
+        pre_v, act_v, grads, grad_sib, grad_chip, got_y, half, swapped, rounded, pieces, final, final_sib,
         local, sent, landed,
     ) = refs
     height, width = feat_flat.shape
@@ -337,34 +337,30 @@
         grad_chip[k] = added[k * side : (k + 1) * side].astype(BF16)
     ring = feats // SIDES
     near, far = lax.rem(mine, ring), mine // ring
-    arrived(back_copies)
     ring_copies = []
     for d in range(1, ring):
         peer = lax.rem(near + d, ring)
         ring_copies.append(
             remote.make(grad_chip.at[:, rows_of(peer)], got_y.at[d - 1], me, far * ring + peer)
         )
+    arrived(back_copies)
     p_dir, p_comb, p_add, p_sib = (out_2.at[k] for k in range(4))
     backward(back, 4 * core, p_dir)
     c_dir = remote.make(p_dir, got_2.at[0], behind, mine)
+    arrived(ring_copies)
+    total = grad_chip[:, rows_of(near)].astype(F32)
+    for d in range(ring - 1):
+        total = total + got_y[d].astype(F32)
+    half[...] = total
+    swap = remote.make(half.at[1 - far], swapped, me, (1 - far) * ring + near)
     backward(back, 1 + 2 * core, p_comb)
     c_comb = remote.make(p_comb, comb_2, sib, mine)
     backward(back, 4 - 4 * core, p_add)
     c_comb.wait_recv()
     p_add[...] = (p_add[...].astype(F32) + comb_2[...].astype(F32)).astype(BF16)
     c_add = remote.make(p_add, got_2.at[1], ahead, mine)
-    arrived(ring_copies)
-    total = grad_chip[:, rows_of(near)].astype(F32)
-    for d in range(ring - 1):
-        total = total + got_y[d].astype(F32)
-    half[...] = total
-    swap = remote.make(half.at[1 - far], swapped, me, (1 - far) * ring + near)
-    backward(back, 3 - 2 * core, p_sib)
-    sums = c_dir, c_add, remote.make(p_sib, got_2.at[2], sib, mine)
-    relays = pass_on(parts, zd_2, relay_2)
-    swap.wait_recv()
-    swapped[...] = swapped[...] + half[far]
-    groups = min(half_nodes, height // 8)
+
+    groups = min(half_nodes, height // 16)
     splits = half_nodes // groups
     tall, wide = height // groups, depth // splits
 
@@ -376,37 +372,37 @@
         )
 
     place = me // 2
-    piece_copies = []
-    for d in range(1, half_nodes):
-        peer = lax.rem(place + d, half_nodes)
-        piece_copies.append(
-            remote.make(
-                swapped.at[piece(peer)], pieces.at[d - 1], 2 * peer + core, mine
-            )
-        )
+    others = [lax.rem(place + d, half_nodes) for d in range(1, half_nodes)]
+    swap.wait_recv()
+    added = swapped[...] + half[far]
+    swapped[...] = added
+    rounded[...] = added.astype(BF16)
+    piece_copies = [
+        remote.make(rounded.at[piece(peer)], pieces.at[d], 2 * peer + core, mine)
+        for d, peer in enumerate(others)
+    ]
+    backward(back, 3 - 2 * core, p_sib)
+    sums = c_dir, c_add, remote.make(p_sib, got_2.at[2], sib, mine)
     c_sb.wait_recv()
     forward(sib_2, 3 - 2 * core)
+    relays = pass_on(parts, zd_2, relay_2)
     arrived(piece_copies)
     total = swapped[piece(place)]
     for d in range(half_nodes - 1):
-        total = total + pieces[d]
+        total = total + pieces[d].astype(F32)
     final[piece(place)] = total
-    final_copies = []
-    for d in range(1, half_nodes):
-        peer = lax.rem(place + d, half_nodes)
-        final_copies.append(
-            remote.make(
-                final.at[piece(place)], final.at[piece(place)], 2 * peer + core, mine
-            )
-        )
+    final_copies = [
+        remote.make(final.at[piece(place)], final.at[piece(place)], 2 * peer + core, mine)
+        for peer in others
+    ]
+    forward(zd_2, 4 - 4 * core)
     c_za.wait_recv()
     forward(za_2, 4 * core)
-    forward(zd_2, 4 - 4 * core)
-    arrived(final_copies)
-    last = remote.make(final, final_sib, sib, mine)
     arrived(relays)
     forward(relay_2, 1 + 2 * core)
     gather_forward(layer_out)
+    arrived(final_copies)
+    last = remote.make(final, final_sib, sib, mine)
     backward(back, 2, own_2)
     last.wait_recv()
     collect(sums, got_2, own_2, feature_grad)
@@ -426,15 +422,9 @@
 
 
 def give_kernel(*refs):
-    half = (len(refs) - 1) // 2
-    copies = [
-        pltpu.make_async_copy(src, dst, refs[-1].at[k])
-        for k, (src, dst) in enumerate(zip(refs[:half], refs[half:-1]))
-    ]
-    for copy in copies:
-        copy.start()
-    for copy in copies:
-        copy.wait()
+    half = len(refs) // 2
+    for src, dst in zip(refs[:half], refs[half:]):
+        dst[...] = src[...]
 
 
 def on_device(features, tiles, tile_rows, tile_cols, counts, weight_one, weight_two, cotangent):
@@ -447,7 +437,7 @@
     share = width // feats
     lanes = -(-max(tile_rows.shape[0], offsets * (width // block)) // 128) * 128
     half_nodes = nodes // 2
-    groups = min(half_nodes, height // 8)
+    groups = min(half_nodes, height // 16)
     piece = (height // groups, depth * groups // half_nodes)
     remote_copies = (
         2 * (2 * CHUNKS + 6) + 4 * (feats - 1) + feats // SIDES - 1 + 3 + 2 * (half_nodes - 1)
@@ -487,7 +477,8 @@
             pltpu.VMEM((max(feats // SIDES - 1, 1), SIDES, height, depth), BF16),
             pltpu.VMEM((SIDES, height, depth), F32),
             pltpu.VMEM((height, depth), F32),
-            pltpu.VMEM((half_nodes - 1, *piece), F32),
+            pltpu.VMEM((height, depth), BF16),
+            pltpu.VMEM((half_nodes - 1, *piece), BF16),
             pltpu.VMEM((height, depth), F32),
             pltpu.VMEM((height, depth), F32),
             pltpu.SemaphoreType.DMA((offsets + 4,)),
@@ -510,9 +501,8 @@
     return pl.pallas_call(
         give_kernel,
         out_shape=[jax.ShapeDtypeStruct(m.shape, m.dtype) for m in made],
-        in_specs=[ANY] * 4,
-        out_specs=[ANY] * 4,
-        scratch_shapes=[pltpu.SemaphoreType.DMA((4,))],
+        in_specs=[VMEM] * 4,
+        out_specs=[VMEM] * 4,
     )(*made)
 
 

time: 156 us -> 111 us (0.71); the launches traced: 154 us -> 111 us
  Pallas kernels: 154 us -> 110 us
    pallas_call x1, Pallas kernels: 40.8 us -> 2.34 us  [on_device(): pl.pallas_call(give_kernel, out_shape=[jax.ShapeDtypeStruct(m.shape, m.dt...]
    pallas_call x1, Pallas kernels: 111 us -> 106 us  [on_device(): pl.pallas_call(functools.partial(kernel, (slots, block, offsets, nodes, f...]
where the time goes in v4:
time: 111 us
  Pallas kernels  110 us (99%)
    pallas_call x1, Pallas kernels, on_device(): pl.pallas_call(functools.partial(kernel, (slots, block, offsets, nodes, f...  106 us
    pallas_call x1, Pallas kernels, on_device(): pl.pallas_call(give_kernel, out_shape=[jax.ShapeDtypeStruct(m.shape, m.dt...  2.34 us

profile of v4, /device:TPU:25, one launch (start us, length us, event | category | flops | bytes accessed | tf_op | source)
XLA Modules:
  0.0 110.9 jit_solution(8317522286425256114)
XLA Ops:
  0.6 1.5 %shard_map.111.refs_2_ = s32[8,256]{1,0:T(8,128)} custom-call(s32[5]{0:T(128)} %counts.1, s32[1,240]{1,0:T(1,128)} %bitcast.2, s32[1,240]{1,0:T(1,128)} %bitcast.3), custom_call_target="tpu_custom_call" | custom-call | tf_op jit(solution)/shard_map/pallas_call | solution.py:451
  2.2 106.4 %shard_map.112 = (bf16[64,4096]{1,0:T(8,128)(2,1)}, bf16[64,4096]{1,0:T(8,128)(2,1)}, f32[64,512]{1,0:T(8,128)}, f32[64,512]{1,0:T(8,128)}) custom-call(s32[240]{0:T(256)} %refs_0_.1, s32[240]{0:T(256)} %refs_1_.1, s32[8,256]{1,0:T(8,128)} %shard_map.111.refs_2_, bf16[64,4096]{1,0:T(8,128)(2,1)} %refs_3_.1, bf16[64,4096]{1,0:T(8,128)(2,1)} %refs_4_.1, ...), custom_call_target="tpu_custom_call" | custom-call | tf_op jit(solution)/shard_map/pallas_call | solution.py:457
  108.5 2.3 %shard_map.113 = (bf16[64,4096]{1,0:T(8,128)(2,1)}, bf16[64,4096]{1,0:T(8,128)(2,1)}, f32[64,512]{1,0:T(8,128)}, f32[64,512]{1,0:T(8,128)}) custom-call(bf16[64,4096]{1,0:T(8,128)(2,1)} %get-tuple-element.8.refs_0_, bf16[64,4096]{1,0:T(8,128)(2,1)} %get-tuple-element.9.refs_1_, f32[64,512]{1,0:T(8,128)} %get-tuple-element.10.refs_2_, ...), custom_call_target="tpu_custom_call" | custom-call | tf_op jit(solution)/shard_map/pallas_call | solution.py:501

commit v5 on v4

--- a/solution.py
+++ b/solution.py
@@ -320,8 +320,6 @@
     sigma = 1.0 / (1.0 + jnp.exp(-pre))
     pre_back = (act_back * sigma * (1.0 + pre * (1.0 - sigma))).astype(BF16)
     put_blocks(dot(one[...], pre_back).astype(BF16), back_send)
-    arrived(up_copies)
-    parts, c_za, c_sb = send_panel(up, za_2, zd_2, sib_2)
     back_copies = to_features(back_send, back)
     grads[0] = lax.dot_general(agg[...], pre_back, TAIL, preferred_element_type=F32).astype(BF16)
     grads[1] = lax.dot_general(
@@ -329,7 +327,11 @@
     ).astype(BF16)
     c_grad = remote.make(grads.at[1 - core], grad_sib, sib, mine)
 
-    forward(up, 2)
+    arrived(up_copies)
+    for copy in back_copies:
+        copy.wait_send()
+    parts, c_za, c_sb = send_panel(up, za_2, zd_2, sib_2)
+
     c_grad.wait_recv()
     side = feats // SIDES * height
     added = grads[core].astype(F32) + grad_sib[...].astype(F32)
@@ -343,23 +345,19 @@
         ring_copies.append(
             remote.make(grad_chip.at[:, rows_of(peer)], got_y.at[d - 1], me, far * ring + peer)
         )
-    arrived(back_copies)
-    p_dir, p_comb, p_add, p_sib = (out_2.at[k] for k in range(4))
-    backward(back, 4 * core, p_dir)
-    c_dir = remote.make(p_dir, got_2.at[0], behind, mine)
+    forward(up, 2)
+    c_sb.wait_recv()
+    forward(sib_2, 3 - 2 * core)
     arrived(ring_copies)
     total = grad_chip[:, rows_of(near)].astype(F32)
     for d in range(ring - 1):
         total = total + got_y[d].astype(F32)
     half[...] = total
     swap = remote.make(half.at[1 - far], swapped, me, (1 - far) * ring + near)
-    backward(back, 1 + 2 * core, p_comb)
-    c_comb = remote.make(p_comb, comb_2, sib, mine)
-    backward(back, 4 - 4 * core, p_add)
-    c_comb.wait_recv()
-    p_add[...] = (p_add[...].astype(F32) + comb_2[...].astype(F32)).astype(BF16)
-    c_add = remote.make(p_add, got_2.at[1], ahead, mine)
-
+    arrived(back_copies)
+    p_dir, p_comb, p_add, p_sib = (out_2.at[k] for k in range(4))
+    backward(back, 4 * core, p_dir)
+    c_dir = remote.make(p_dir, got_2.at[0], behind, mine)
     groups = min(half_nodes, height // 16)
     splits = half_nodes // groups
     tall, wide = height // groups, depth // splits
@@ -381,11 +379,13 @@
         remote.make(rounded.at[piece(peer)], pieces.at[d], 2 * peer + core, mine)
         for d, peer in enumerate(others)
     ]
-    backward(back, 3 - 2 * core, p_sib)
-    sums = c_dir, c_add, remote.make(p_sib, got_2.at[2], sib, mine)
-    c_sb.wait_recv()
-    forward(sib_2, 3 - 2 * core)
-    relays = pass_on(parts, zd_2, relay_2)
+    backward(back, 1 + 2 * core, p_comb)
+    c_comb = remote.make(p_comb, comb_2, sib, mine)
+    backward(back, 4 - 4 * core, p_add)
+    c_comb.wait_recv()
+    p_add[...] = (p_add[...].astype(F32) + comb_2[...].astype(F32)).astype(BF16)
+    c_add = remote.make(p_add, got_2.at[1], ahead, mine)
+
     arrived(piece_copies)
     total = swapped[piece(place)]
     for d in range(half_nodes - 1):
@@ -395,6 +395,9 @@
         remote.make(final.at[piece(place)], final.at[piece(place)], 2 * peer + core, mine)
         for peer in others
     ]
+    backward(back, 3 - 2 * core, p_sib)
+    sums = c_dir, c_add, remote.make(p_sib, got_2.at[2], sib, mine)
+    relays = pass_on(parts, zd_2, relay_2)
     forward(zd_2, 4 - 4 * core)
     c_za.wait_recv()
     forward(za_2, 4 * core)

time: 111 us -> 106 us (0.955)
  Pallas kernels: 110 us -> 105 us
    pallas_call x1, Pallas kernels: 106 us -> 101 us  [on_device(): pl.pallas_call(functools.partial(kernel, (slots, block, offsets, nodes, f...]
where the time goes in v5:
time: 106 us; the launch traced here: 105 us
  Pallas kernels  105 us (99%)
    pallas_call x1, Pallas kernels, on_device(): pl.pallas_call(functools.partial(kernel, (slots, block, offsets, nodes, f...  101 us
    pallas_call x1, Pallas kernels, on_device(): pl.pallas_call(give_kernel, out_shape=[jax.ShapeDtypeStruct(m.shape, m.dt...  2.34 us

profile of v5, /device:TPU:25, one launch (start us, length us, event | category | flops | bytes accessed | tf_op | source)
XLA Modules:
  0.0 105.3 jit_solution(3678317882613144524)
XLA Ops:
  0.6 1.5 %shard_map.111.refs_2_ = s32[8,256]{1,0:T(8,128)} custom-call(s32[5]{0:T(128)} %counts.1, s32[1,240]{1,0:T(1,128)} %bitcast.2, s32[1,240]{1,0:T(1,128)} %bitcast.3), custom_call_target="tpu_custom_call" | custom-call | tf_op jit(solution)/shard_map/pallas_call | solution.py:454
  2.2 100.8 %shard_map.112 = (bf16[64,4096]{1,0:T(8,128)(2,1)}, bf16[64,4096]{1,0:T(8,128)(2,1)}, f32[64,512]{1,0:T(8,128)}, f32[64,512]{1,0:T(8,128)}) custom-call(s32[240]{0:T(256)} %refs_0_.1, s32[240]{0:T(256)} %refs_1_.1, s32[8,256]{1,0:T(8,128)} %shard_map.111.refs_2_, bf16[64,4096]{1,0:T(8,128)(2,1)} %refs_3_.1, bf16[64,4096]{1,0:T(8,128)(2,1)} %refs_4_.1, ...), custom_call_target="tpu_custom_call" | custom-call | tf_op jit(solution)/shard_map/pallas_call | solution.py:460
  102.9 2.3 %shard_map.113 = (bf16[64,4096]{1,0:T(8,128)(2,1)}, bf16[64,4096]{1,0:T(8,128)(2,1)}, f32[64,512]{1,0:T(8,128)}, f32[64,512]{1,0:T(8,128)}) custom-call(bf16[64,4096]{1,0:T(8,128)(2,1)} %get-tuple-element.8.refs_0_, bf16[64,4096]{1,0:T(8,128)(2,1)} %get-tuple-element.9.refs_1_, f32[64,512]{1,0:T(8,128)} %get-tuple-element.10.refs_2_, ...), custom_call_target="tpu_custom_call" | custom-call | tf_op jit(solution)/shard_map/pallas_call | solution.py:504
